TPU v7x, 128 devices: a whole 4x4x4 slice. The times are simulated.
128 devices in a mesh: grp: 8 (over x, y_hi), blk: 16 (over y_lo, z, core).
Axes of the slice: x: 4, y: 4 (y_hi: 2, y_lo: 2; y = y_hi * 2 + y_lo), z: 4, core: 2. Of those that a mesh axis runs over, the one named last changes fastest.
Arguments:
- fluid_temp: float32 [256, 512, 768], P('grp', 'blk'), may hold values from -6 to 6
- velocity: float32 [3, 256, 512, 768], P(None, 'grp', 'blk'), may hold values from -0.5 to 0.5
- solid_temp: float32 [64, 128, 768], P('grp', 'blk'), may hold values from -6 to 6
- conductivity: float32 [3, 64, 128, 768], P(None, 'grp', 'blk'), may hold values from 0.5 to 4
- face_fluid_cell: int32 [8, 32768], P('grp', 'blk'), may hold values from 0 to 786431
- face_owner: int32 [8, 32768], P('grp', 'blk'), may hold values from 0 to 15, as said below
- face_solid_cell: int32 [8, 32768], P('grp', 'blk'), may hold values from 0 to 49151
- face_conductance: float32 [8, 32768], P('grp', 'blk'), may hold values from 0.5 to 2
Outputs:
- fluid_next: float32 [256, 512, 768], P('grp', 'blk')
- solid_next: float32 [64, 128, 768], P('grp', 'blk')
Inputs may be any that keep to these rules, and one draw needn't show every extreme that they name: `face_owner`: among the rows of one device each owner appears at most 512 times; in each index of grp one owner appears exactly 512 times among the rows of every device of that index.
All inputs are finite; a program needn't handle non-finite values.
Results may differ from a plain program's by a relative error of at most 0.0003.
Values sent between devices are 32-bit elements; how exact they have to be, the bound alone decides.
A program may use at most 128 MiB of HBM per device.

v0:
```python
import math

import jax
import jax.numpy as jnp
from jax import lax
from jax.sharding import PartitionSpec as P

SLOTS = 512
SWEEPS = 4


time_step = 0.2
diffusivity = 0.2
capacity = 0.5


def padded_2(cells, sides, width):
    for axis, dim in sides:
        count = lax.axis_size(axis)
        ends = count - 1
        head = lax.slice_in_dim(cells, 0, width, axis=dim)
        tail = lax.slice_in_dim(cells, cells.shape[dim] - width, cells.shape[dim], axis=dim)
        cells = jnp.concatenate(
            [
                lax.ppermute(tail, axis, [(i, (i + 1) % count) for i in range(ends)]),
                cells,
                lax.ppermute(head, axis, [((i + 1) % count, i) for i in range(ends)]),
            ],
            axis=dim,
        )
    return cells


def owner_ranks(onehot):
    count_rows = onehot.shape[0]
    width = math.gcd(count_rows, 128)
    grouped = onehot.reshape(count_rows // width, width, onehot.shape[1])
    lower_ones = (jnp.arange(width)[:, None] >= jnp.arange(width)[None, :]).astype(jnp.float32)
    inside = jnp.einsum("ij,kjb->kib", lower_ones, grouped, precision=lax.Precision.HIGHEST)
    totals = inside[:, -1, :]
    offsets = jnp.cumsum(totals, axis=0) - totals
    running = (inside + offsets[:, None, :]).reshape(count_rows, onehot.shape[1])
    return (jnp.sum(running * onehot, axis=1) - 1.0).astype(jnp.int32)


def shards(
    fluid_temp,
    velocity,
    solid_temp,
    conductivity,
    face_fluid_cell,
    face_owner,
    face_solid_cell,
    face_conductance,
):
    blocks = lax.axis_size("blk")
    face_cells = face_fluid_cell[0]
    owners = face_owner[0]
    targets = face_solid_cell[0]
    conduct = face_conductance[0]
    onehot = (owners[:, None] == jnp.arange(blocks, dtype=jnp.int32)[None, :]).astype(jnp.float32)
    ranks = owner_ranks(onehot)
    fluid_flat = fluid_temp.reshape(-1)
    face_temp = fluid_flat[face_cells]

    def place(values):
        return jnp.zeros((blocks, SLOTS), jnp.float32).at[owners, ranks].set(values)

    outgoing = jnp.stack(
        [place(face_temp), place(conduct), place(targets.astype(jnp.float32))], axis=1
    )
    incoming = lax.all_to_all(outgoing, "blk", split_axis=0, concat_axis=0, tiled=True)
    wall_flat = solid_temp.reshape(-1)
    slot_cells = incoming[:, 2, :].astype(jnp.int32)
    fluxes = incoming[:, 1, :] * (incoming[:, 0, :] - wall_flat[slot_cells])
    deposit = jnp.zeros_like(wall_flat).at[slot_cells.reshape(-1)].add(fluxes.reshape(-1))
    deposit = deposit.reshape(solid_temp.shape)
    returned = lax.all_to_all(fluxes, "blk", split_axis=0, concat_axis=0, tiled=True)
    face_flux = returned[owners, ranks]
    fields = jnp.concatenate([fluid_temp[None], velocity], axis=0)
    padded_all = padded_2(fields, (("grp", 1), ("blk", 2)), 1)
    padded_all = jnp.pad(padded_all, ((0, 0), (0, 0), (0, 0), (1, 1)))
    padded = padded_all[0]
    flow_x = padded_all[1]
    flow_y = padded_all[2]
    flow_z = padded_all[3]
    speeds = [
        (
            0.5 * (flow_x[:-2, 1:-1, 1:-1] + flow_x[1:-1, 1:-1, 1:-1]),
            0.5 * (flow_x[1:-1, 1:-1, 1:-1] + flow_x[2:, 1:-1, 1:-1]),
        ),
        (
            0.5 * (flow_y[1:-1, :-2, 1:-1] + flow_y[1:-1, 1:-1, 1:-1]),
            0.5 * (flow_y[1:-1, 1:-1, 1:-1] + flow_y[1:-1, 2:, 1:-1]),
        ),
        (
            0.5 * (flow_z[1:-1, 1:-1, :-2] + flow_z[1:-1, 1:-1, 1:-1]),
            0.5 * (flow_z[1:-1, 1:-1, 1:-1] + flow_z[1:-1, 1:-1, 2:]),
        ),
    ]
    centre = padded[1:-1, 1:-1, 1:-1]
    lows = [padded[:-2, 1:-1, 1:-1], padded[1:-1, :-2, 1:-1], padded[1:-1, 1:-1, :-2]]
    highs = [padded[2:, 1:-1, 1:-1], padded[1:-1, 2:, 1:-1], padded[1:-1, 1:-1, 2:]]
    change = jnp.zeros_like(fluid_temp)
    for axis_number in range(3):
        low_speed, high_speed = speeds[axis_number]
        lower = lows[axis_number]
        upper = highs[axis_number]
        inflow = jnp.maximum(low_speed, 0.0) * lower + jnp.minimum(low_speed, 0.0) * centre
        outflow = jnp.maximum(high_speed, 0.0) * centre + jnp.minimum(high_speed, 0.0) * upper
        change = change + (inflow - outflow) + diffusivity * (upper + lower - 2.0 * centre)
    advanced = (fluid_temp + time_step * change).reshape(-1)
    fluid_next = advanced.at[face_cells].add(-time_step * face_flux).reshape(fluid_temp.shape)
    divisor = capacity + 2.0 * (conductivity[0] + conductivity[1] + conductivity[2])
    base = capacity * solid_temp + deposit
    current = solid_temp
    for sweep in range(SWEEPS):
        beside_all = padded_2(current, (("grp", 0), ("blk", 1)), 1)
        beside_all = jnp.pad(beside_all, ((0, 0), (0, 0), (1, 1)))
        beside = conductivity[0] * (beside_all[2:, 1:-1, 1:-1] + beside_all[:-2, 1:-1, 1:-1])
        beside = beside + conductivity[1] * (
            beside_all[1:-1, 2:, 1:-1] + beside_all[1:-1, :-2, 1:-1]
        )
        beside = beside + conductivity[2] * (
            beside_all[1:-1, 1:-1, 2:] + beside_all[1:-1, 1:-1, :-2]
        )
        current = (base + beside) / divisor
    return (fluid_next, current)


def solution(mesh):
    in_specs = (
        P("grp", "blk", None),
        P(None, "grp", "blk", None),
        P("grp", "blk", None),
        P(None, "grp", "blk", None),
        P("grp", "blk"),
        P("grp", "blk"),
        P("grp", "blk"),
        P("grp", "blk"),
    )
    out_specs = (P("grp", "blk", None), P("grp", "blk", None))
    return jax.shard_map(shards, mesh=mesh, in_specs=in_specs, out_specs=out_specs, check_vma=False)
```

profile of v0, /device:TPU:14, one launch (start us, length us, event | category | flops | bytes accessed | tf_op | source)
XLA Modules:
  0.0 366.1 jit_solution(12929221116720132950)
XLA Ops:
  0.6 0.8 fusion.64
  1.4 4.2 %collective-permute-start.5 = (f32[1,8,768]{2,1,0:T(8,128)S(1)}, f32[1,8,768]{2,1,0:T(8,128)S(1)}, u32[]{:S(2)}, u32[]{:S(2)}) collective-permute-start(f32[1,8,768]{2,1,0:T(8,128)S(1)} %get-tuple-element.25), channel_id=1, source_target_pairs={{0,16},{16,32},{32,48},{48,64},{64,80},{80,96},{96,112},{1,17},{17... | collective-permute-start | bytes 73736 | tf_op jit(solution)/shard_map/ppermute | solution.py:25
  5.6 4.0 %collective-permute-start.4 = (f32[1,8,768]{2,1,0:T(8,128)S(1)}, f32[1,8,768]{2,1,0:T(8,128)S(1)}, u32[]{:S(2)}, u32[]{:S(2)}) collective-permute-start(f32[1,8,768]{2,1,0:T(8,128)S(1)} %get-tuple-element.24), channel_id=1, source_target_pairs={{16,0},{32,16},{48,32},{64,48},{80,64},{96,80},{112,96},{17,1},{33... | collective-permute-start | bytes 73736 | tf_op jit(solution)/shard_map/ppermute | solution.py:27
  9.6 0.7 compare_select_fusion.4
  10.4 0.9 convolution_bitcast_fusion
  11.9 0.8 select_reduce_fusion
  12.7 0.7 shift-left_or_fusion
  13.5 0.8 and_reduce_fusion
  14.2 0.7 multiply_reduce_fusion
  15.0 0.7 convert_element_type.54
  15.7 8.1 %scatter_custom_fusion.4 = f32[8192]{0:T(1024)S(1)} fusion(s32[2048]{0:T(1024)S(1)} %broadcast_select_fusion, f32[2048]{0:T(1024)S(1)} %bitcast.101, f32[]{:T(128)} %constant.11.clone.1), kind=kCustom, calls=%fused_computation.164 | custom fusion | bytes 32772
  23.8 8.2 %scatter_custom_fusion.3 = f32[8192]{0:T(1024)S(1)} fusion(s32[2048]{0:T(1024)S(1)} %broadcast_select_fusion, f32[2048]{0:T(1024)} %bitcast.102, f32[]{:T(128)} %constant.11.clone.1), kind=kCustom, calls=%fused_computation.166 | custom fusion | bytes 33280
  32.0 2.7 reshape.175
  34.7 11.8 %gather_fusion = f32[2048]{0:T(1024)S(1)} fusion(f32[786432]{0:T(1024)S(1)} %reshape.175, s32[2048]{0:T(1024)S(1)} %broadcast_clamp_fusion.1), kind=kCustom, calls=%fused_computation | custom fusion | bytes 24576 | tf_op jit(solution)/shard_map/gather | solution.py:64
  46.5 8.1 %scatter_custom_fusion.2 = f32[8192]{0:T(1024)S(1)} fusion(s32[2048]{0:T(1024)S(1)} %broadcast_select_fusion, f32[2048]{0:T(1024)S(1)} %gather_fusion, f32[]{:T(128)} %constant.11.clone.1), kind=kCustom, calls=%fused_computation.168 | custom fusion | bytes 32772
  54.8 4.7 %collective-permute-start.6 = (f32[10,1,768]{2,1,0:T(1,128)S(1)}, f32[10,1,768]{2,1,0:T(1,128)S(1)}, u32[]{:S(2)}, u32[]{:S(2)}) collective-permute-start(f32[10,1,768]{2,1,0:T(1,128)S(1)} %get-tuple-element.17), channel_id=1, source_target_pairs={{1,0},{2,1},{3,2},{4,3},{5,4},{6,5},{7,6},{8,7},{9,8},{10,9},{11,1... | collective-permute-start | bytes 92168 | tf_op jit(solution)/shard_map/ppermute | solution.py:27
  59.5 1.9 collective-permute-start.7
  61.4 0.7 pad_maximum_fusion.34
  62.2 5.7 %all-to-all-start = ((f32[16,3,512]{2,1,0:T(4,128)}), f32[16,3,512]{2,1,0:T(4,128)S(1)}, u32[]{:S(2)}, u32[]{:S(2)}) async-start(f32[16,3,512]{2,1,0:T(4,128)} %pad_maximum_fusion.34), calls=%async_computation | async-start | bytes 262144 | tf_op jit(solution)/shard_map/all_to_all | solution.py:72
  67.9 1.2 select_maximum_fusion.17
  69.1 4.1 %all-to-all-done = f32[16,3,512]{2,1,0:T(4,128)S(1)} async-done(((f32[16,3,512]{2,1,0:T(4,128)}), f32[16,3,512]{2,1,0:T(4,128)S(1)}, u32[]{:S(2)}, u32[]{:S(2)}) %all-to-all-start) | async-done | bytes 98336 | tf_op jit(solution)/shard_map/all_to_all | solution.py:72
  73.2 45.5 %gather_fusion.1 = f32[8192]{0:T(1024)S(1)} fusion(f32[49152]{0:T(1024)S(1)} %reshape.176, s32[8192]{0:T(1024)S(1)} %broadcast_clamp_fusion), kind=kCustom, calls=%fused_computation.1 | custom fusion | bytes 98304 | tf_op jit(solution)/shard_map/gather | solution.py:75
  118.8 0.7 fusion.65
  119.5 0.6 subtract_multiply_fusion
  120.1 55.3 %scatter_custom_fusion.1 = f32[49152]{0:T(1024)} fusion(s32[8192]{0:T(1024)S(1)} %bitcast.100, f32[8192]{0:T(1024)} %subtract_multiply_fusion, f32[]{:T(128)} %constant.11.clone.1), kind=kCustom, calls=%fused_computation.140 | custom fusion | flops 8192 | bytes 197120 | tf_op jit(solution)/shard_map/scatter-add | solution.py:76
  175.4 1.7 reshape.178
  177.1 1.9 fusion.41
  179.0 3.9 %collective-permute-start.8 = (f32[1,8,768]{2,1,0:T(8,128)S(1)}, f32[1,8,768]{2,1,0:T(8,128)S(1)}, u32[]{:S(2)}, u32[]{:S(2)}) collective-permute-start(f32[1,8,768]{2,1,0:T(8,128)S(1)} %get-tuple-element.23), channel_id=1, source_target_pairs={{16,0},{32,16},{48,32},{64,48},{80,64},{96,80},{112,96},{17,1},{33... | collective-permute-start | bytes 73736 | tf_op jit(solution)/shard_map/ppermute | solution.py:27
  182.8 3.5 collective-permute-start.9
  186.3 4.6 %collective-permute-done.9 = f32[1,8,768]{2,1,0:T(8,128)S(1)} collective-permute-done((f32[1,8,768]{2,1,0:T(8,128)S(1)}, f32[1,8,768]{2,1,0:T(8,128)S(1)}, u32[]{:S(2)}, u32[]{:S(2)}) %collective-permute-start.9) | collective-permute-done | bytes 24608 | tf_op jit(solution)/shard_map/ppermute | solution.py:25
  191.0 2.8 collective-permute-start.10
  193.8 1.9 collective-permute-start.11
  195.8 5.4 %collective-permute-done.11 = f32[10,1,768]{2,1,0:T(1,128)S(1)} collective-permute-done((f32[10,1,768]{2,1,0:T(1,128)S(1)}, f32[10,1,768]{2,1,0:T(1,128)S(1)}, u32[]{:S(2)}, u32[]{:S(2)}) %collective-permute-start.11) | collective-permute-done | bytes 30752 | tf_op jit(solution)/shard_map/ppermute | solution.py:25
  201.8 2.0 collective-permute-start.12
  203.8 5.4 %collective-permute-start.13 = (f32[1,8,768]{2,1,0:T(8,128)S(1)}, f32[1,8,768]{2,1,0:T(8,128)S(1)}, u32[]{:S(2)}, u32[]{:S(2)}) collective-permute-start(f32[1,8,768]{2,1,0:T(8,128)S(1)} %get-tuple-element.20), channel_id=1, source_target_pairs={{0,16},{16,32},{32,48},{48,64},{64,80},{80,96},{96,112},{1,17},{17... | collective-permute-start | bytes 73736 | tf_op jit(solution)/shard_map/ppermute | solution.py:25
  209.2 2.7 collective-permute-done.13
  211.9 0.7 pad_maximum_fusion.38
  212.6 1.9 collective-permute-start.14
  214.5 2.4 collective-permute-start.15
  216.9 2.0 pad_maximum_fusion.5
  218.9 4.5 %collective-permute-start.1 = (f32[4,1,32,768]{3,2,1,0:T(8,128)}, f32[4,1,32,768]{3,2,1,0:T(8,128)}, u32[]{:S(2)}, u32[]{:S(2)}) collective-permute-start(f32[4,1,32,768]{3,2,1,0:T(8,128)} %get-tuple-element.9), channel_id=1, source_target_pairs={{16,0},{32,16},{48,32},{64,48},{80,64},{96,80},{112,96},{17,1},{33... | collective-permute-start | bytes 1179656 | tf_op jit(solution)/shard_map/ppermute | solution.py:27
  223.4 3.6 collective-permute-start
  227.0 4.7 %all-to-all-start.1 = ((f32[16,1,512]{2,1,0:T(1,128)}), f32[16,1,512]{2,1,0:T(1,128)S(1)}, u32[]{:S(2)}, u32[]{:S(2)}) async-start(f32[16,1,512]{2,1,0:T(1,128)} %get-tuple-element.27), calls=%async_computation.1 | async-start | bytes 65536 | tf_op jit(solution)/shard_map/all_to_all | solution.py:78
  231.7 1.3 select_maximum_fusion.9
  233.0 1.7 fusion.23
  234.7 0.7 copy-done.6
  235.4 4.6 %collective-permute-start.16 = (f32[1,8,768]{2,1,0:T(8,128)S(1)}, f32[1,8,768]{2,1,0:T(8,128)S(1)}, u32[]{:S(2)}, u32[]{:S(2)}) collective-permute-start(f32[1,8,768]{2,1,0:T(8,128)S(1)} %get-tuple-element.19), channel_id=1, source_target_pairs={{16,0},{32,16},{48,32},{64,48},{80,64},{96,80},{112,96},{17,1},{33... | collective-permute-start | bytes 73736 | tf_op jit(solution)/shard_map/ppermute | solution.py:27
  240.0 2.7 collective-permute-start.17
  242.8 16.6 %gather_fusion.2 = f32[2048]{0:T(1024)S(1)} fusion(f32[16,512]{1,0:T(8,128)S(1)} %bitcast.80, s32[2048]{0:T(1024)S(1)} %bitcast.81), kind=kCustom, calls=%fused_computation.2 | custom fusion | bytes 32768 | tf_op jit(solution)/shard_map/gather | solution.py:79
  259.4 1.1 pad_maximum_fusion.35
  260.5 3.8 %collective-permute-start.18 = (f32[10,1,768]{2,1,0:T(1,128)S(1)}, f32[10,1,768]{2,1,0:T(1,128)S(1)}, u32[]{:S(2)}, u32[]{:S(2)}) collective-permute-start(f32[10,1,768]{2,1,0:T(1,128)S(1)} %get-tuple-element.11), channel_id=1, source_target_pairs={{1,0},{2,1},{3,2},{4,3},{5,4},{6,5},{7,6},{8,7},{9,8},{10,9},{11,1... | collective-permute-start | bytes 92168 | tf_op jit(solution)/shard_map/ppermute | solution.py:27
  264.4 2.3 collective-permute-start.19
  266.8 3.5 pad_maximum_fusion.3
  270.4 5.0 %collective-permute-start.3 = (f32[4,34,1,768]{3,1,2,0:T(8,128)S(1)}, f32[4,34,1,768]{3,1,2,0:T(8,128)S(1)}, u32[]{:S(2)}, u32[]{:S(2)}) collective-permute-start(f32[4,34,1,768]{3,1,2,0:T(8,128)S(1)} %copy.26), channel_id=1, source_target_pairs={{1,0},{2,1},{3,2},{4,3},{5,4},{6,5},{7,6},{8,7},{9,8},{10,9},{11,1... | collective-permute-start | bytes 1253384 | tf_op jit(solution)/shard_map/ppermute | solution.py:27
  275.4 2.1 collective-permute-start.2
  277.9 0.9 fusion.14
  278.8 2.8 collective-permute-done.3
  282.1 5.5 %collective-permute-done.2 = f32[4,34,1,768]{3,1,2,0:T(8,128)S(1)} collective-permute-done((f32[4,34,1,768]{3,1,2,0:T(8,128)S(1)}, f32[4,34,1,768]{3,1,2,0:T(8,128)S(1)}, u32[]{:S(2)}, u32[]{:S(2)}) %collective-permute-start.2) | collective-permute-done | bytes 417824 | tf_op jit(solution)/shard_map/ppermute | solution.py:25
  288.1 28.1 %select_maximum_fusion = f32[4,34,34,770]{3,2,1,0:T(8,128)} fusion(f32[4,34,1,768]{3,2,1,0:T(1,128)S(1)} %copy.28, f32[4,34,1,768]{3,2,1,0:T(1,128)S(1)} %copy.27, f32[4,1,32,768]{3,2,1,0:T(8,128)} %collective-permute-done.1, f32[4,1,32,768]{3,2,1,0:T(8,128)} %collective-permute-done, f32[3,32,32,768]{3,2,1,0:T(8,128)S(1)} %bitcast.83, ...), kind=kLoop, calls=%fused_computation.10 | loop fusion | flops 49846720 | bytes 28446848 | tf_op jit(solution)/shard_map/concatenate | solution.py:23
  316.2 11.3 %slice_bitcast_fusion.3 = (f32[34,34,770]{2,1,0:T(8,128)S(1)}, f32[34,34,770]{2,1,0:T(8,128)}, f32[34,34,770]{2,1,0:T(8,128)S(1)}, f32[34,34,770]{2,1,0:T(8,128)}) fusion(f32[4,34,34,770]{3,2,1,0:T(8,128)} %select_maximum_fusion), kind=kLoop, calls=%fused_computation.19 | loop fusion | bytes 28483840 | tf_op jit(solution)/shard_map/squeeze | solution.py:84
  327.5 21.3 %multiply_add_fusion = f32[32,32,768]{2,1,0:T(8,128)} fusion(f32[32,32,768]{2,1,0:T(8,128)S(1)} %copy-done, f32[34,34,770]{2,1,0:T(8,128)S(1)} %get-tuple-element.4, f32[34,34,770]{2,1,0:T(8,128)} %get-tuple-element.5, f32[34,34,770]{2,1,0:T(8,128)} %get-tuple-element.3, f32[34,34,770]{2,1,0:T(8,128)S(1)} %get-tuple-element.2), kind=kLoop, calls=%fused_computation.32 | loop fusion | flops 48758784 | bytes 56623104 | tf_op jit(solution)/shard_map/add | solution.py:112
  348.8 2.7 reshape.174
  351.5 12.6 %scatter_fusion = f32[786432]{0:T(1024)S(1)} fusion(f32[786432]{0:T(1024)S(1)} %reshape.174, s32[2048]{0:T(1024)S(1)} %bitcast.96, f32[2048]{0:T(1024)S(1)} %broadcast_multiply_fusion), kind=kCustom, calls=%fused_computation.3 | custom fusion | flops 2048 | bytes 32768 | tf_op jit(solution)/shard_map/scatter-add | solution.py:113
  364.1 2.0 reshape.177
  (71 shorter events, 2.9 us)
Async XLA Ops:
  1.4 53.2 %collective-permute-start.5 = (f32[1,8,768]{2,1,0:T(8,128)S(1)}, f32[1,8,768]{2,1,0:T(8,128)S(1)}, u32[]{:S(2)}, u32[]{:S(2)}) collective-permute-start(f32[1,8,768]{2,1,0:T(8,128)S(1)} %get-tuple-element.25), channel_id=1, source_target_pairs={{0,16},{16,32},{32,48},{48,64},{64,80},{80,96},{96,112},{1,17},{17... | collective-permute-start | bytes 73736 | tf_op jit(solution)/shard_map/ppermute | solution.py:25
  5.6 49.1 %collective-permute-start.4 = (f32[1,8,768]{2,1,0:T(8,128)S(1)}, f32[1,8,768]{2,1,0:T(8,128)S(1)}, u32[]{:S(2)}, u32[]{:S(2)}) collective-permute-start(f32[1,8,768]{2,1,0:T(8,128)S(1)} %get-tuple-element.24), channel_id=1, source_target_pairs={{16,0},{32,16},{48,32},{64,48},{80,64},{96,80},{112,96},{17,1},{33... | collective-permute-start | bytes 73736 | tf_op jit(solution)/shard_map/ppermute | solution.py:27
  34.7 19.9 %copy-start.3 = (f32[8,8,768]{2,1,0:T(8,128)S(1)}, f32[8,8,768]{2,1,0:T(8,128)}, u32[]{:S(2)}) copy-start(f32[8,8,768]{2,1,0:T(8,128)} %param.10) | copy-start | bytes 589828
  54.7 64.1 %copy-start.9 = (f32[10,8,768]{2,1,0:T(8,128)}, f32[10,8,768]{2,1,0:T(8,128)S(1)}, u32[]{:S(2)}) copy-start(f32[10,8,768]{2,1,0:T(8,128)S(1)} %constant_dynamic-update-slice_fusion) | copy-start | bytes 737284
  54.8 13.1 %collective-permute-start.6 = (f32[10,1,768]{2,1,0:T(1,128)S(1)}, f32[10,1,768]{2,1,0:T(1,128)S(1)}, u32[]{:S(2)}, u32[]{:S(2)}) collective-permute-start(f32[10,1,768]{2,1,0:T(1,128)S(1)} %get-tuple-element.17), channel_id=1, source_target_pairs={{1,0},{2,1},{3,2},{4,3},{5,4},{6,5},{7,6},{8,7},{9,8},{10,9},{11,1... | collective-permute-start | bytes 92168 | tf_op jit(solution)/shard_map/ppermute | solution.py:27
  59.5 8.4 %collective-permute-start.7 = (f32[10,1,768]{2,1,0:T(1,128)S(1)}, f32[10,1,768]{2,1,0:T(1,128)S(1)}, u32[]{:S(2)}, u32[]{:S(2)}) collective-permute-start(f32[10,1,768]{2,1,0:T(1,128)S(1)} %get-tuple-element.16), channel_id=1, source_target_pairs={{0,1},{1,2},{2,3},{3,4},{4,5},{5,6},{6,7},{7,8},{8,9},{9,10},{10,1... | collective-permute-start | bytes 92168 | tf_op jit(solution)/shard_map/ppermute | solution.py:25
  62.2 11.0 %all-to-all-start = ((f32[16,3,512]{2,1,0:T(4,128)}), f32[16,3,512]{2,1,0:T(4,128)S(1)}, u32[]{:S(2)}, u32[]{:S(2)}) async-start(f32[16,3,512]{2,1,0:T(4,128)} %pad_maximum_fusion.34), calls=%async_computation | async-start | bytes 262144 | tf_op jit(solution)/shard_map/all_to_all | solution.py:72
  119.5 97.4 %copy-start = (f32[32,32,768]{2,1,0:T(8,128)S(1)}, f32[32,32,768]{2,1,0:T(8,128)}, u32[]{:S(2)}) copy-start(f32[32,32,768]{2,1,0:T(8,128)} %param.8) | copy-start | bytes 9437188
  177.1 24.5 %copy-start.1 = (f32[3,8,8,768]{3,2,1,0:T(8,128)S(1)}, f32[3,8,8,768]{3,2,1,0:T(8,128)}, u32[]{:S(2)}) copy-start(f32[3,8,8,768]{3,2,1,0:T(8,128)} %param.11) | copy-start | bytes 1769476
  177.1 24.5 %copy-start.4 = (f32[8,8,768]{2,1,0:T(8,128)S(1)}, f32[8,8,768]{2,1,0:T(8,128)}, u32[]{:S(2)}) copy-start(f32[8,8,768]{2,1,0:T(8,128)} %reshape.178) | copy-start | bytes 589828
  179.0 7.4 %collective-permute-start.8 = (f32[1,8,768]{2,1,0:T(8,128)S(1)}, f32[1,8,768]{2,1,0:T(8,128)S(1)}, u32[]{:S(2)}, u32[]{:S(2)}) collective-permute-start(f32[1,8,768]{2,1,0:T(8,128)S(1)} %get-tuple-element.23), channel_id=1, source_target_pairs={{16,0},{32,16},{48,32},{64,48},{80,64},{96,80},{112,96},{17,1},{33... | collective-permute-start | bytes 73736 | tf_op jit(solution)/shard_map/ppermute | solution.py:27
  182.8 8.1 %collective-permute-start.9 = (f32[1,8,768]{2,1,0:T(8,128)S(1)}, f32[1,8,768]{2,1,0:T(8,128)S(1)}, u32[]{:S(2)}, u32[]{:S(2)}) collective-permute-start(f32[1,8,768]{2,1,0:T(8,128)S(1)} %get-tuple-element.22), channel_id=1, source_target_pairs={{0,16},{16,32},{32,48},{48,64},{64,80},{80,96},{96,112},{1,17},{17... | collective-permute-start | bytes 73736 | tf_op jit(solution)/shard_map/ppermute | solution.py:25
  191.0 4.8 %collective-permute-start.10 = (f32[10,1,768]{2,1,0:T(1,128)S(1)}, f32[10,1,768]{2,1,0:T(1,128)S(1)}, u32[]{:S(2)}, u32[]{:S(2)}) collective-permute-start(f32[10,1,768]{2,1,0:T(1,128)S(1)} %get-tuple-element.15), channel_id=1, source_target_pairs={{1,0},{2,1},{3,2},{4,3},{5,4},{6,5},{7,6},{8,7},{9,8},{10,9},{11,1... | collective-permute-start | bytes 92168 | tf_op jit(solution)/shard_map/ppermute | solution.py:27
  193.8 7.3 %collective-permute-start.11 = (f32[10,1,768]{2,1,0:T(1,128)S(1)}, f32[10,1,768]{2,1,0:T(1,128)S(1)}, u32[]{:S(2)}, u32[]{:S(2)}) collective-permute-start(f32[10,1,768]{2,1,0:T(1,128)S(1)} %get-tuple-element.14), channel_id=1, source_target_pairs={{0,1},{1,2},{2,3},{3,4},{4,5},{5,6},{6,7},{7,8},{8,9},{9,10},{10,1... | collective-permute-start | bytes 92168 | tf_op jit(solution)/shard_map/ppermute | solution.py:25
  201.8 17.1 %copy-start.8 = (f32[8,8,768]{2,1,0:T(8,128)}, f32[8,8,768]{2,1,0:T(8,128)S(1)}, u32[]{:S(2)}) copy-start(f32[8,8,768]{2,1,0:T(8,128)S(1)} %fusion.32) | copy-start | bytes 589828
  201.8 7.4 %collective-permute-start.12 = (f32[1,8,768]{2,1,0:T(8,128)S(1)}, f32[1,8,768]{2,1,0:T(8,128)S(1)}, u32[]{:S(2)}, u32[]{:S(2)}) collective-permute-start(f32[1,8,768]{2,1,0:T(8,128)S(1)} %get-tuple-element.21), channel_id=1, source_target_pairs={{16,0},{32,16},{48,32},{64,48},{80,64},{96,80},{112,96},{17,1},{33... | collective-permute-start | bytes 73736 | tf_op jit(solution)/shard_map/ppermute | solution.py:27
  203.8 8.1 %collective-permute-start.13 = (f32[1,8,768]{2,1,0:T(8,128)S(1)}, f32[1,8,768]{2,1,0:T(8,128)S(1)}, u32[]{:S(2)}, u32[]{:S(2)}) collective-permute-start(f32[1,8,768]{2,1,0:T(8,128)S(1)} %get-tuple-element.20), channel_id=1, source_target_pairs={{0,16},{16,32},{32,48},{48,64},{64,80},{80,96},{96,112},{1,17},{17... | collective-permute-start | bytes 73736 | tf_op jit(solution)/shard_map/ppermute | solution.py:25
  212.6 19.1 %collective-permute-start.14 = (f32[10,1,768]{2,1,0:T(1,128)}, f32[10,1,768]{2,1,0:T(1,128)S(1)}, u32[]{:S(2)}, u32[]{:S(2)}) collective-permute-start(f32[10,1,768]{2,1,0:T(1,128)} %get-tuple-element.13), channel_id=1, source_target_pairs={{1,0},{2,1},{3,2},{4,3},{5,4},{6,5},{7,6},{8,7},{9,8},{10,9},{11,1... | collective-permute-start | bytes 92168 | tf_op jit(solution)/shard_map/ppermute | solution.py:27
  214.5 17.2 %collective-permute-start.15 = (f32[10,1,768]{2,1,0:T(1,128)}, f32[10,1,768]{2,1,0:T(1,128)S(1)}, u32[]{:S(2)}, u32[]{:S(2)}) collective-permute-start(f32[10,1,768]{2,1,0:T(1,128)} %get-tuple-element.12), channel_id=1, source_target_pairs={{0,1},{1,2},{2,3},{3,4},{4,5},{5,6},{6,7},{7,8},{8,9},{9,10},{10,1... | collective-permute-start | bytes 92168 | tf_op jit(solution)/shard_map/ppermute | solution.py:25
  218.9 47.8 %collective-permute-start.1 = (f32[4,1,32,768]{3,2,1,0:T(8,128)}, f32[4,1,32,768]{3,2,1,0:T(8,128)}, u32[]{:S(2)}, u32[]{:S(2)}) collective-permute-start(f32[4,1,32,768]{3,2,1,0:T(8,128)} %get-tuple-element.9), channel_id=1, source_target_pairs={{16,0},{32,16},{48,32},{64,48},{80,64},{96,80},{112,96},{17,1},{33... | collective-permute-start | bytes 1179656 | tf_op jit(solution)/shard_map/ppermute | solution.py:27
  223.4 43.4 %collective-permute-start = (f32[4,1,32,768]{3,2,1,0:T(8,128)}, f32[4,1,32,768]{3,2,1,0:T(8,128)}, u32[]{:S(2)}, u32[]{:S(2)}) collective-permute-start(f32[4,1,32,768]{3,2,1,0:T(8,128)} %get-tuple-element.8), channel_id=1, source_target_pairs={{0,16},{16,32},{32,48},{48,64},{64,80},{80,96},{96,112},{1,17},{17... | collective-permute-start | bytes 1179656 | tf_op jit(solution)/shard_map/ppermute | solution.py:25
  227.0 15.7 %all-to-all-start.1 = ((f32[16,1,512]{2,1,0:T(1,128)}), f32[16,1,512]{2,1,0:T(1,128)S(1)}, u32[]{:S(2)}, u32[]{:S(2)}) async-start(f32[16,1,512]{2,1,0:T(1,128)} %get-tuple-element.27), calls=%async_computation.1 | async-start | bytes 65536 | tf_op jit(solution)/shard_map/all_to_all | solution.py:78
  234.7 0.7 copy-start.6
  235.4 24.0 %collective-permute-start.16 = (f32[1,8,768]{2,1,0:T(8,128)S(1)}, f32[1,8,768]{2,1,0:T(8,128)S(1)}, u32[]{:S(2)}, u32[]{:S(2)}) collective-permute-start(f32[1,8,768]{2,1,0:T(8,128)S(1)} %get-tuple-element.19), channel_id=1, source_target_pairs={{16,0},{32,16},{48,32},{64,48},{80,64},{96,80},{112,96},{17,1},{33... | collective-permute-start | bytes 73736 | tf_op jit(solution)/shard_map/ppermute | solution.py:27
  240.0 19.4 %collective-permute-start.17 = (f32[1,8,768]{2,1,0:T(8,128)S(1)}, f32[1,8,768]{2,1,0:T(8,128)S(1)}, u32[]{:S(2)}, u32[]{:S(2)}) collective-permute-start(f32[1,8,768]{2,1,0:T(8,128)S(1)} %get-tuple-element.18), channel_id=1, source_target_pairs={{0,16},{16,32},{32,48},{48,64},{64,80},{80,96},{96,112},{1,17},{17... | collective-permute-start | bytes 73736 | tf_op jit(solution)/shard_map/ppermute | solution.py:25
  260.5 17.0 %collective-permute-start.18 = (f32[10,1,768]{2,1,0:T(1,128)S(1)}, f32[10,1,768]{2,1,0:T(1,128)S(1)}, u32[]{:S(2)}, u32[]{:S(2)}) collective-permute-start(f32[10,1,768]{2,1,0:T(1,128)S(1)} %get-tuple-element.11), channel_id=1, source_target_pairs={{1,0},{2,1},{3,2},{4,3},{5,4},{6,5},{7,6},{8,7},{9,8},{10,9},{11,1... | collective-permute-start | bytes 92168 | tf_op jit(solution)/shard_map/ppermute | solution.py:27
  264.4 23.7 %slice-start = ((s8[9437184]{0:T(1024)(128)(4,1)}), s8[4194304]{0:T(1024)(128)(4,1)S(1)}, s32[]{:S(2)}) async-start(s8[9437184]{0:T(1024)(128)(4,1)} %bitcast.82), calls=%async_computation.2 | async-start | bytes 8388608
  264.4 13.2 %copy-start.7 = (f32[8,8,768]{2,1,0:T(8,128)S(1)}, f32[8,8,768]{2,1,0:T(8,128)}, u32[]{:S(2)}) copy-start(f32[8,8,768]{2,1,0:T(8,128)} %copy-done.6) | copy-start | bytes 589828
  264.4 13.5 %copy-start.2 = (f32[3,8,8,768]{3,2,1,0:T(8,128)S(1)}, f32[3,8,8,768]{3,2,1,0:T(8,128)}, u32[]{:S(2)}) copy-start(f32[3,8,8,768]{3,2,1,0:T(8,128)} %param.11) | copy-start | bytes 1769476
  264.4 13.5 %copy-start.5 = (f32[8,8,768]{2,1,0:T(8,128)S(1)}, f32[8,8,768]{2,1,0:T(8,128)}, u32[]{:S(2)}) copy-start(f32[8,8,768]{2,1,0:T(8,128)} %reshape.178) | copy-start | bytes 589828
  264.4 23.7 %slice-start.1 = ((s8[9437184]{0:T(1024)(128)(4,1)}), s8[4194304]{0:T(1024)(128)(4,1)S(1)}, s32[]{:S(2)}) async-start(s8[9437184]{0:T(1024)(128)(4,1)} %bitcast.82), calls=%async_computation.3 | async-start | bytes 8388608
  264.4 23.7 %slice-start.2 = ((s8[9437184]{0:T(1024)(128)(4,1)}), s8[1048576]{0:T(1024)(128)(4,1)S(1)}, s32[]{:S(2)}) async-start(s8[9437184]{0:T(1024)(128)(4,1)} %bitcast.82), calls=%async_computation.4 | async-start | bytes 2097152
  264.4 13.1 %collective-permute-start.19 = (f32[10,1,768]{2,1,0:T(1,128)S(1)}, f32[10,1,768]{2,1,0:T(1,128)S(1)}, u32[]{:S(2)}, u32[]{:S(2)}) collective-permute-start(f32[10,1,768]{2,1,0:T(1,128)S(1)} %get-tuple-element.10), channel_id=1, source_target_pairs={{0,1},{1,2},{2,3},{3,4},{4,5},{5,6},{6,7},{7,8},{8,9},{9,10},{10,1... | collective-permute-start | bytes 92168 | tf_op jit(solution)/shard_map/ppermute | solution.py:25
  270.4 11.3 %collective-permute-start.3 = (f32[4,34,1,768]{3,1,2,0:T(8,128)S(1)}, f32[4,34,1,768]{3,1,2,0:T(8,128)S(1)}, u32[]{:S(2)}, u32[]{:S(2)}) collective-permute-start(f32[4,34,1,768]{3,1,2,0:T(8,128)S(1)} %copy.26), channel_id=1, source_target_pairs={{1,0},{2,1},{3,2},{4,3},{5,4},{6,5},{7,6},{8,7},{9,8},{10,9},{11,1... | collective-permute-start | bytes 1253384 | tf_op jit(solution)/shard_map/ppermute | solution.py:27
  275.4 12.3 %collective-permute-start.2 = (f32[4,34,1,768]{3,1,2,0:T(8,128)S(1)}, f32[4,34,1,768]{3,1,2,0:T(8,128)S(1)}, u32[]{:S(2)}, u32[]{:S(2)}) collective-permute-start(f32[4,34,1,768]{3,1,2,0:T(8,128)S(1)} %copy.25), channel_id=1, source_target_pairs={{0,1},{1,2},{2,3},{3,4},{4,5},{5,6},{6,7},{7,8},{8,9},{9,10},{10,1... | collective-permute-start | bytes 1253384 | tf_op jit(solution)/shard_map/ppermute | solution.py:25
where the time goes:
time: 369 us; the launch traced here: 366 us
  other arithmetic  139 us (38%)
  local copies, waits for them, and re-layouts  122 us (33%)
  starting transfers between devices  77.6 us (21%)
  waiting for transfers between devices  25.2 us (7%)
    scatter-add x1, other arithmetic, shards(): jnp.zeros_like(wall_flat).at[slot_cells.reshape(-1)].add(fluxes.reshape(-1))  55.3 us
    gather x1, local copies, waits for them, and re-layouts, shards(): fluxes = incoming[:, 1, :] * (incoming[:, 0, :] - wall_flat[slot_cells])  45.5 us
    ppermute x10, starting transfers between devices, padded_2(): lax.ppermute(head, axis, [((i + 1) % count, i) for i in range(ends)])  37.2 us
    concatenate x8, other arithmetic, padded_2(): jnp.concatenate([lax.ppermute(tail, axis, [(i, (i + 1) % count) for i in...  33.1 us
    ppermute x10, starting transfers between devices, padded_2(): lax.ppermute(tail, axis, [(i, (i + 1) % count) for i in range(ends)])  30.1 us
    unnamed x32, local copies, waits for them, and re-layouts  25.2 us
    add x1, other arithmetic, shards(): advanced = (fluid_temp + time_step * change).reshape(-1)  21.3 us
    ppermute x10, waiting for transfers between devices, padded_2(): lax.ppermute(tail, axis, [(i, (i + 1) % count) for i in range(ends)])  18.3 us
  transfers between devices with their start and end apart: 22, of which 6 were waited for; matrix products, arithmetic and copies ran while one was open for 20% of the time, Pallas kernels for 0%

commit v1 on v0

v1 whole, which is shorter than its diff:
```python
import jax
import jax.numpy as jnp
from jax import lax
from jax.experimental import pallas as pl
from jax.experimental.pallas import tpu as pltpu
from jax.sharding import PartitionSpec as P

F32 = jnp.float32
BF = jnp.bfloat16
I32 = jnp.int32
MESH = pl.DeviceIdType.MESH

NX, NY, NZ = 32, 32, 768
WX, WY = 8, 8
ZB = NZ // 128
SLOTS = 512
FACES = 2048
GRP, BLK = 8, 16
ROWS = WX * WY * ZB


def split3(v):
    hi = v.astype(BF).astype(F32)
    rest = v - hi
    mid = rest.astype(BF).astype(F32)
    return hi, mid, rest - mid


def dot(a, b):
    return lax.dot_general(a, b, (((1,), (0,)), ((), ())), preferred_element_type=F32)


def dot_nt(a, b):
    return lax.dot_general(a, b, (((1,), (1,)), ((), ())), preferred_element_type=F32)


def onehot(index, count):
    rows = lax.broadcasted_iota(I32, (count, index.shape[1]), 0)
    return jnp.where(rows == index, 1.0, 0.0).astype(BF)


def face(a, b, va, vb):
    s = 0.1 * (va + vb)
    return b * s + (jnp.maximum(s, 0.0) + 0.04) * (a - b)


def shift_up(v, lane):
    r = pltpu.roll(v, 1, 1)
    first = jnp.where(lane == 0, 0.0, r[:, :128])
    return jnp.concatenate([first, r[:, 128:]], axis=1)


def shift_down(v, lane, last):
    r = pltpu.roll(v, v.shape[1] - 1, 1)
    top = jnp.where(lane == 127, last, r[:, -128:])
    return jnp.concatenate([r[:, :-128], top], axis=1)


def main_kernel(
    rows_s, cell_v, owner_v, code_v, cond_v, fluid, vel, solid, kond,
    adv_out, solid_out, flux_out,
    tg, tp, vyp, vxp, vz, adv, buf, tf_s, rank_s, snd, inc, flx, ret, rmat,
    ysnd, yrcv, cur, sysnd, syrcv, kp, inv, base, table, dep, gs, gxs,
    lsem, ssem, rsem, osem, isem, fsem, bsem,
):
    g = lax.axis_index("grp")
    b = lax.axis_index("blk")
    has = {("g", 0): g > 0, ("g", 1): g < GRP - 1, ("b", 0): b > 0, ("b", 1): b < BLK - 1}

    def neighbour(axis, side):
        step = 1 if side else -1
        return (g + step, b) if axis == "g" else (g, b + step)

    loads = []

    def load(src, dst):
        c = pltpu.make_async_copy(src, dst, lsem.at[len(loads)])
        c.start()
        loads.append(c)

    for zb in range(ZB):
        load(fluid.at[:, :, pl.ds(zb * 128, 128)], tg.at[zb])
    load(fluid, tp.at[pl.ds(1, NX), pl.ds(8, NY), :])
    load(vel.at[1], vyp.at[:, pl.ds(8, NY), :])
    load(solid, cur.at[0, pl.ds(1, WX), pl.ds(8, WY), :])
    load(vel.at[0], vxp.at[pl.ds(1, NX)])
    load(vel.at[2], vz)
    load(kond, kp)

    bar = pltpu.get_barrier_semaphore()

    def greet(k, carry):
        pl.semaphore_signal(bar, inc=1, device_id=(g, lax.rem(b + k, BLK)), device_id_type=MESH)
        return carry

    lax.fori_loop(1, BLK, greet, 0)
    for side in (0, 1):
        @pl.when(has["g", side])
        def _():
            pl.semaphore_signal(bar, inc=1, device_id=neighbour("g", side), device_id_type=MESH)

    for side in (0, 1):
        @pl.when(jnp.logical_not(has["g", side]))
        def _():
            at = 0 if side == 0 else NX + 1
            tp[at, 8:40, :] = jnp.zeros((NY, NZ), F32)
            vxp[at] = jnp.zeros((NY, NZ), F32)
            wat = 0 if side == 0 else WX + 1
            for k in range(4):
                cur[k, wat, 8:16, :] = jnp.zeros((WY, NZ), F32)

        @pl.when(jnp.logical_not(has["b", side]))
        def _():
            yrcv[side] = jnp.zeros((2, NX, NZ), F32)
            for k in range(4):
                syrcv[k, side] = jnp.zeros((WX, NZ), F32)

    owner = owner_v[...]
    own16 = onehot(owner, BLK)
    upper = jnp.where(
        lax.broadcasted_iota(I32, (128, 128), 0) <= lax.broadcasted_iota(I32, (128, 128), 1), 1.0, 0.0
    ).astype(BF)
    offset = jnp.zeros((BLK, 1), F32)
    for c in range(FACES // 128):
        mine = own16[:, c * 128:(c + 1) * 128]
        running = dot(mine, upper) + offset
        offset = running[:, 127:128]
        rank_s[:, c * 128:(c + 1) * 128] = (
            jnp.sum(jnp.where(mine.astype(F32) > 0.5, running, 0.0), axis=0, keepdims=True) - 1.0
        ).astype(I32)

    def remote(src, dst, at, device):
        return pltpu.make_async_remote_copy(
            src_ref=src, dst_ref=dst, send_sem=ssem.at[at], recv_sem=rsem.at[at],
            device_id=device, device_id_type=MESH,
        )

    def message(kind, axis, k=0):
        out = []
        for slot in (0, 1):
            side = 1 - slot
            to = neighbour(axis, side)
            if kind == "t":
                c = remote(fluid.at[NX - 1 if side else 0],
                           tp.at[NX + 1 if slot else 0, pl.ds(8, NY), :], slot, to)
            elif kind == "v":
                c = remote(vel.at[0, NX - 1 if side else 0], vxp.at[NX + 1 if slot else 0], 2 + slot, to)
            elif kind == "y":
                c = remote(ysnd.at[side], yrcv.at[slot], 4 + slot, to)
            elif kind == "sx":
                c = remote(cur.at[k, WX if side else 1, pl.ds(8, WY), :],
                           cur.at[k, WX + 1 if slot else 0, pl.ds(8, WY), :], 6 + 2 * k + slot, to)
            else:
                c = remote(sysnd.at[k, side], syrcv.at[k, slot], 14 + 2 * k + slot, to)
            out.append(c)
        return out

    def send(kind, axis, k=0):
        for slot, c in enumerate(message(kind, axis, k)):
            @pl.when(has[axis, 1 - slot])
            def _():
                c.start()

    def receive(kind, axis, k=0):
        for slot, c in enumerate(message(kind, axis, k)):
            @pl.when(has[axis, slot])
            def _():
                c.wait_recv()

    def sent(kind, axis, k=0):
        for slot, c in enumerate(message(kind, axis, k)):
            @pl.when(has[axis, 1 - slot])
            def _():
                c.wait_send()

    greeted = 15 + has["g", 0].astype(I32) + has["g", 1].astype(I32)
    pl.semaphore_wait(bar, greeted)

    send("t", "g")
    send("v", "g")
    for i in (6, 7):
        loads[i].wait()

    def pack(x, carry):
        ysnd[0, 0, pl.ds(x, 1), :] = tp[x + 1, 8:9, :]
        ysnd[1, 0, pl.ds(x, 1), :] = tp[x + 1, 39:40, :]
        ysnd[0, 1, pl.ds(x, 1), :] = vyp[x, 8:9, :]
        ysnd[1, 1, pl.ds(x, 1), :] = vyp[x, 39:40, :]
        return carry

    lax.fori_loop(0, NX, pack, 0)
    send("y", "b")
    loads[8].wait()

    def solid_send(k):
        for x in range(WX):
            sysnd[k, 0, x:x + 1, :] = cur[k, x + 1, 8:9, :]
            sysnd[k, 1, x:x + 1, :] = cur[k, x + 1, 15:16, :]
        send("sx", "g", k)
        send("sy", "b", k)

    def solid_receive(k):
        receive("sx", "g", k)
        receive("sy", "b", k)
        for x in range(WX):
            cur[k, x + 1, 7:8, :] = syrcv[k, 0, x:x + 1, :]
            cur[k, x + 1, 16:17, :] = syrcv[k, 1, x:x + 1, :]

    solid_send(0)

    for i in range(ZB):
        loads[i].wait()
    flat = tg.reshape(ZB * NX * NY, 128)

    def gather(i, carry):
        at = pl.multiple_of(i * 16, 16)
        for u in range(16):
            buf[pl.ds(at + u, 1), :] = flat[pl.ds(rows_s[0, at + u], 1), :]
        return carry

    lax.fori_loop(0, FACES // 16, gather, 0)
    lane128 = lax.broadcasted_iota(I32, (128, 128), 0)
    for c in range(FACES // 128):
        cols = slice(c * 128, (c + 1) * 128)
        block = buf[cols, :].T
        lane = cell_v[:, cols] & 127
        tf_s[:, cols] = jnp.sum(jnp.where(lane128 == lane, block, 0.0), axis=0, keepdims=True)

    code = code_v[...]
    fields = jnp.concatenate(
        list(split3(tf_s[...])) + list(split3(cond_v[...]))
        + [((code >> 8) << 8).astype(F32), (code & 255).astype(F32)], axis=0)
    many = jnp.concatenate([fields] * BLK, axis=0)
    to = lax.broadcasted_iota(I32, (8 * BLK, FACES), 0) >> 3
    many = jnp.where(to == owner, many, 0.0).astype(BF)
    placed = dot_nt(many, onehot(rank_s[...], SLOTS))
    two = placed + pltpu.roll(placed, 8 * BLK - 1, 0)
    three = two + pltpu.roll(placed, 8 * BLK - 2, 0)
    which = lax.broadcasted_iota(I32, (8 * BLK, SLOTS), 0) & 7
    snd[...] = jnp.where(which == 6, two, three)

    def row_copy(k):
        to = lax.rem(b + k, BLK)
        return pltpu.make_async_remote_copy(
            src_ref=snd.at[pl.ds(pl.multiple_of(to * 8, 8), 8), :],
            dst_ref=inc.at[pl.ds(pl.multiple_of(b * 8, 8), 8), :],
            send_sem=osem.at[k], recv_sem=isem.at[k], device_id=(g, to), device_id_type=MESH)

    def flux_copy(k):
        to = lax.rem(b + BLK - k, BLK)
        return pltpu.make_async_remote_copy(
            src_ref=flx.at[to], dst_ref=ret.at[b],
            send_sem=fsem.at[k], recv_sem=bsem.at[k], device_id=(g, to), device_id_type=MESH)

    def row_send(k, carry):
        row_copy(k).start()
        return carry

    lax.fori_loop(1, BLK, row_send, 0)

    lane = lax.broadcasted_iota(I32, (8, 128), 1)
    loads[11].wait()
    for x in range(WX):
        k0, k1, k2 = kp[0, x], kp[1, x], kp[2, x]
        r = 1.0 / (0.5 + 2.0 * (k0 + k1 + k2))
        inv[x] = r
        kp[0, x] = k0 * r
        kp[1, x] = k1 * r
        kp[2, x] = k2 * r
    for zb in range(ZB):
        for x in range(WX):
            at = zb * 64 + x * 8
            dep[at:at + 8, 0:128] = cur[0, x + 1, 8:16, zb * 128:(zb + 1) * 128]
    across = dep[:, 0:128].T
    for i, part in enumerate(split3(across)):
        table[i * 128:(i + 1) * 128, :] = part.astype(BF)
    dep[...] = jnp.zeros((ROWS, 256), F32)

    def low_x(x):
        for t in range(4):
            r = 8 * t
            gxs[r:r + 8, :] = face(tp[x, 8 + r:16 + r, :], tp[x + 1, 8 + r:16 + r, :],
                                   vxp[x, r:r + 8, :], vxp[x + 1, r:r + 8, :])

    def slab(x, carry):
        for t in range(4):
            r = 8 + 8 * t
            gs[8 * t:8 * t + 8, :] = face(tp[x + 1, r - 1:r + 7, :], tp[x + 1, r:r + 8, :],
                                          vyp[x, r - 1:r + 7, :], vyp[x, r:r + 8, :])
        gs[32:33, :] = face(tp[x + 1, 39:40, :], tp[x + 1, 40:41, :], vyp[x, 39:40, :], vyp[x, 40:41, :])
        for t in range(4):
            r = 8 * t
            here = tp[x + 1, r + 8:r + 16, :]
            high = face(here, tp[x + 2, r + 8:r + 16, :], vxp[x + 1, r:r + 8, :], vxp[x + 2, r:r + 8, :])
            low = gxs[r:r + 8, :]
            gxs[r:r + 8, :] = high
            v = vz[x, r:r + 8, :]
            bottom = face(shift_up(here, lane), here, shift_up(v, lane), v)
            last = face(here[:, -128:], 0.0, v[:, -128:], 0.0)
            top = shift_down(bottom, lane, last)
            adv[x, r:r + 8, :] = (here + (low - high) + (gs[r:r + 8, :] - gs[r + 1:r + 9, :])
                                  + (bottom - top))
        return carry

    def spread(x, carry):
        tp[x + 1, 7:8, :] = yrcv[0, 0, pl.ds(x, 1), :]
        tp[x + 1, 40:41, :] = yrcv[1, 0, pl.ds(x, 1), :]
        vyp[x, 7:8, :] = yrcv[0, 1, pl.ds(x, 1), :]
        vyp[x, 40:41, :] = yrcv[1, 1, pl.ds(x, 1), :]
        return carry

    receive("y", "b")
    lax.fori_loop(0, NX, spread, 0)
    loads[9].wait()
    loads[10].wait()
    low_x(1)
    lax.fori_loop(1, 6, slab, 0)

    pl_own = pl.ds(pl.multiple_of(b * 8, 8), 8)
    inc[pl_own, :] = snd[pl_own, :]

    def work(k):
        src = lax.rem(b + BLK - k, BLK)
        at = pl.multiple_of(src * 8, 8)
        temp = inc[pl.ds(at, 8), :]
        code = temp[6:7, :].astype(I32)
        hot = onehot(code >> 7, ROWS)
        mask = lax.broadcasted_iota(I32, (128, SLOTS), 0) == (code & 127)
        found = dot(table[...], hot)
        found = found[0:128] + found[128:256] + found[256:384]
        wall = jnp.sum(jnp.where(mask, found, 0.0), axis=0, keepdims=True)
        flux = temp[3:4, :] * (temp[0:1, :] - wall)
        flx[src] = flux
        hi = flux.astype(BF).astype(F32)
        spread = jnp.concatenate([jnp.where(mask, hi, 0.0), jnp.where(mask, flux - hi, 0.0)], axis=0)
        dep[...] += dot_nt(hot, spread.astype(BF))

    work(0)

    def owned(k, carry):
        row_copy(k).wait_recv()
        work(k)
        flux_copy(k).start()
        return carry

    lax.fori_loop(1, BLK, owned, 0)

    def sweep(k, x):
        here = cur[k, x + 1, 8:16, :]
        beside = kp[0, x] * (cur[k, x + 2, 8:16, :] + cur[k, x, 8:16, :])
        beside = beside + kp[1, x] * (cur[k, x + 1, 9:17, :] + cur[k, x + 1, 7:15, :])
        beside = beside + kp[2, x] * (shift_up(here, lane) + shift_down(here, lane, 0.0))
        return base[x] + beside

    solid_receive(0)
    for x in range(WX):
        deposit = jnp.concatenate(
            [dep[zb * 64 + x * 8:zb * 64 + x * 8 + 8, 0:128] + dep[zb * 64 + x * 8:zb * 64 + x * 8 + 8, 128:256]
             for zb in range(ZB)], axis=1)
        base[x] = (0.5 * cur[0, x + 1, 8:16, :] + deposit) * inv[x]
        cur[1, x + 1, 8:16, :] = sweep(0, x)
    solid_send(1)
    lax.fori_loop(6, 15, slab, 0)
    solid_receive(1)
    for x in range(WX):
        cur[2, x + 1, 8:16, :] = sweep(1, x)
    solid_send(2)
    lax.fori_loop(15, 24, slab, 0)
    solid_receive(2)
    for x in range(WX):
        cur[3, x + 1, 8:16, :] = sweep(2, x)
    solid_send(3)
    lax.fori_loop(24, 31, slab, 0)
    receive("t", "g")
    receive("v", "g")
    slab(31, 0)
    low_x(0)
    slab(0, 0)
    out = pltpu.make_async_copy(adv, adv_out, lsem.at[12])
    out.start()

    own_at = pl.ds(b, 1)
    ret[own_at] = flx[own_at]

    def returned(k, carry):
        flux_copy(k).wait_recv()
        return carry

    lax.fori_loop(1, BLK, returned, 0)
    for j in range(BLK):
        rmat[j:j + 1, :] = ret[j]
    stacked = jnp.concatenate(list(split3(rmat[...])), axis=0).astype(BF)
    back = dot(stacked, onehot(rank_s[...], SLOTS))
    back = back[0:16] + back[16:32] + back[32:48]
    own = lax.broadcasted_iota(I32, (BLK, FACES), 0) == owner
    flux_out[...] = jnp.sum(jnp.where(own, back, 0.0), axis=0, keepdims=True)

    solid_receive(3)
    for x in range(WX):
        solid_out[x] = sweep(3, x)

    def drained(k, carry):
        row_copy(k).wait_send()
        flux_copy(k).wait_send()
        return carry

    lax.fori_loop(1, BLK, drained, 0)
    sent("t", "g")
    sent("v", "g")
    sent("y", "b")
    for k in range(4):
        sent("sx", "g", k)
        sent("sy", "b", k)
    out.wait()


def sink_kernel(flux_v, cell_v, adv, out, weights, rowcode):
    step = pl.program_id(0)
    slabs = adv.shape[0]

    @pl.when(step == 0)
    def _():
        cell = cell_v[...]
        coarse = cell >> 8
        xy = (coarse * 43691) >> 17
        zb = (cell >> 7) - 6 * xy
        rowcode[...] = (xy >> 5) * 192 + zb * 32 + (xy & 31)
        mask = lax.broadcasted_iota(I32, (128, FACES), 0) == (cell & 127)
        flux = -0.2 * flux_v[...]
        hi = flux.astype(BF).astype(F32)
        weights[0:128, :] = jnp.where(mask, hi, 0.0).astype(BF)
        weights[128:256, :] = jnp.where(mask, flux - hi, 0.0).astype(BF)

    hot = onehot(rowcode[...] - step * (slabs * 192), slabs * 192)
    total = dot_nt(hot, weights[...])
    total = total[:, 0:128] + total[:, 128:256]
    for x in range(slabs):
        for zb in range(ZB):
            at = x * 192 + zb * 32
            cols = slice(zb * 128, (zb + 1) * 128)
            out[x, :, cols] = adv[x, :, cols] + total[at:at + 32, :]


def shards(fluid, vel, solid, kond, cell, owner, target, cond):
    coarse = cell >> 8
    xy = (coarse * 43691) >> 17
    rows = ((cell >> 7) - 6 * xy) * (NX * NY) + xy
    wxy = ((target >> 8) * 43691) >> 17
    code = (((target >> 7) - 6 * wxy) * (WX * WY) + wxy) * 128 + (target & 127)
    vmem = pl.BlockSpec(memory_space=pltpu.VMEM)
    any_ = pl.BlockSpec(memory_space=pl.ANY)
    dma = pltpu.SemaphoreType.DMA
    adv, solid_next, flux = pl.pallas_call(
        main_kernel,
        out_shape=(
            jax.ShapeDtypeStruct((NX, NY, NZ), F32),
            jax.ShapeDtypeStruct((WX, WY, NZ), F32),
            jax.ShapeDtypeStruct((1, FACES), F32),
        ),
        in_specs=[pl.BlockSpec(memory_space=pltpu.SMEM)] + [vmem] * 4 + [any_] * 4,
        out_specs=(any_, vmem, vmem),
        scratch_shapes=[
            pltpu.VMEM((ZB, NX, NY, 128), F32),
            pltpu.VMEM((NX + 2, NY + 16, NZ), F32),
            pltpu.VMEM((NX, NY + 16, NZ), F32),
            pltpu.VMEM((NX + 2, NY, NZ), F32),
            pltpu.VMEM((NX, NY, NZ), F32),
            pltpu.VMEM((NX, NY, NZ), F32),
            pltpu.VMEM((FACES, 128), F32),
            pltpu.VMEM((1, FACES), F32),
            pltpu.VMEM((1, FACES), I32),
            pltpu.VMEM((8 * BLK, SLOTS), F32),
            pltpu.VMEM((8 * BLK, SLOTS), F32),
            pltpu.VMEM((BLK, 1, SLOTS), F32),
            pltpu.VMEM((BLK, 1, SLOTS), F32),
            pltpu.VMEM((BLK, SLOTS), F32),
            pltpu.VMEM((2, 2, NX, NZ), F32),
            pltpu.VMEM((2, 2, NX, NZ), F32),
            pltpu.VMEM((4, WX + 2, 24, NZ), F32),
            pltpu.VMEM((4, 2, WX, NZ), F32),
            pltpu.VMEM((4, 2, WX, NZ), F32),
            pltpu.VMEM((3, WX, WY, NZ), F32),
            pltpu.VMEM((WX, WY, NZ), F32),
            pltpu.VMEM((WX, WY, NZ), F32),
            pltpu.VMEM((3 * 128, ROWS), BF),
            pltpu.VMEM((ROWS, 256), F32),
            pltpu.VMEM((40, NZ), F32),
            pltpu.VMEM((NY, NZ), F32),
            dma((13,)), dma((22,)), dma((22,)), dma((BLK,)), dma((BLK,)), dma((BLK,)), dma((BLK,)),
        ],
        compiler_params=pltpu.CompilerParams(
            collective_id=0, has_side_effects=True, vmem_limit_bytes=60 * 1024 * 1024),
        name="exchange",
    )(rows, cell, owner, code, cond, fluid, vel, solid, kond)
    slabs = 4
    block = pl.BlockSpec((slabs, NY, NZ), lambda i: (i, 0, 0))
    row = pl.BlockSpec((1, FACES), lambda i: (0, 0))
    fluid_next = pl.pallas_call(
        sink_kernel,
        grid=(NX // slabs,),
        out_shape=jax.ShapeDtypeStruct((NX, NY, NZ), F32),
        in_specs=[row, row, block],
        out_specs=block,
        scratch_shapes=[pltpu.VMEM((256, FACES), BF), pltpu.VMEM((1, FACES), I32)],
        name="sink",
    )(flux, cell, adv)
    return fluid_next, solid_next


def solution(mesh):
    in_specs = (
        P("grp", "blk", None),
        P(None, "grp", "blk", None),
        P("grp", "blk", None),
        P(None, "grp", "blk", None),
        P("grp", "blk"),
        P("grp", "blk"),
        P("grp", "blk"),
        P("grp", "blk"),
    )
    out_specs = (P("grp", "blk", None), P("grp", "blk", None))
    return jax.shard_map(shards, mesh=mesh, in_specs=in_specs, out_specs=out_specs, check_vma=False)
```

time: 369 us -> 64.4 us (0.17)
  other arithmetic: 139 us -> 1.36 us
  local copies, waits for them, and re-layouts: 122 us -> 0.68 us
  starting transfers between devices: 77.6 us -> 0 us
  Pallas kernels: 0 us -> 61.2 us
  waiting for transfers between devices: 25.2 us -> 0 us
    gather x3 -> x0, local copies, waits for them, and re-layouts: 74 us -> none  [the longest x1 45.5 us: shards(): fluxes = incoming[:, 1, :] * (incoming[:, 0, :] - wall_flat[slot_cells])]
    scatter-add x2 -> x0, other arithmetic: 67.9 us -> none  [the longest x1 55.3 us: shards(): jnp.zeros_like(wall_flat).at[slot_cells.reshape(-1)].add(fluxes.reshape(-1))]
    ppermute x20 -> x0, starting transfers between devices: 67.2 us -> none  [the longest x10 37.2 us: padded_2(): lax.ppermute(head, axis, [((i + 1) % count, i) for i in range(ends)])]
    pallas_call x0 -> x2, Pallas kernels: none -> 61.2 us  [the longest x1 50.6 us: shards(): pl.pallas_call(main_kernel, out_shape=(jax.ShapeDtypeStruct((NX, NY, NZ),...]
    concatenate x9 -> x0, other arithmetic: 33.8 us -> none  [the longest x8 33.1 us: padded_2(): jnp.concatenate([lax.ppermute(tail, axis, [(i, (i + 1) % count) for i in...]
    unnamed x32 -> x3, local copies, waits for them, and re-layouts: 25.2 us -> 0.68 us
    ppermute x20 -> x0, waiting for transfers between devices: 21.1 us -> none  [the longest x10 18.3 us: padded_2(): lax.ppermute(tail, axis, [(i, (i + 1) % count) for i in range(ends)])]
    add x1, other arithmetic: 21.3 us -> 1.36 us  [shards(): code = (((target >> 7) - 6 * wxy) * (WX * WY) + wxy) * 128 + (target & 127)]
  transfers between devices with their start and end apart: 22 -> 0, of which waited for: 6 -> 0; matrix products, arithmetic and copies ran while one was open for 20% -> 0% of each run, Pallas kernels for 0% -> 0%
where the time goes in v1:
time: 64.4 us; the launch traced here: 63.9 us
  Pallas kernels  61.2 us (95%)
  other arithmetic  1.36 us (2%)
  local copies, waits for them, and re-layouts  0.68 us (1%)
  between operations  0.65 us (1%)
    pallas_call x1, Pallas kernels, shards(): pl.pallas_call(main_kernel, out_shape=(jax.ShapeDtypeStruct((NX, NY, NZ),...  50.6 us
    pallas_call x1, Pallas kernels, shards(): pl.pallas_call(sink_kernel, grid=(NX // slabs,), out_shape=jax.ShapeDtype...  10.7 us
    add x1, other arithmetic, shards(): code = (((target >> 7) - 6 * wxy) * (WX * WY) + wxy) * 128 + (target & 127)  1.36 us

profile of v1, /device:TPU:14, one launch (start us, length us, event | category | flops | bytes accessed | tf_op | source)
XLA Modules:
  0.0 63.9 jit_solution(755527767513790213)
XLA Ops:
  0.6 1.4 %and_add_fusion = (s32[1,2048]{1,0:T(1,128)}, s32[1,2048]{1,0:T(1,128)}) fusion(s32[1,2048]{1,0:T(1,128)} %param.14, s32[1,2048]{1,0:T(1,128)} %cell_v.3), kind=kLoop, calls=%fused_computation | loop fusion | flops 38912 | bytes 32768 | tf_op jit(solution)/shard_map/add | solution.py:449
  2.0 50.6 %exchange.1 = (f32[32,32,768]{2,1,0:T(8,128)}, f32[8,8,768]{2,1,0:T(8,128)}, f32[1,2048]{1,0:T(1,128)}) custom-call(s32[1,2048]{1,0:T(1,128)} %get-tuple-element.9.rows_s, s32[1,2048]{1,0:T(1,128)} %cell_v.3, s32[1,2048]{1,0:T(1,128)} %owner_v.1, s32[1,2048]{1,0:T(1,128)} %get-tuple-element.8.code_v, f32[1,2048]{1,0:T(1,128)} %cond_v.1, ...), custom_call_target="tpu_custom_call" | custom-call | tf_op jit(solution)/shard_map/exchange/pallas_call | solution.py:453
  52.6 0.0 copy-start
  52.6 10.7 %sink.1 = f32[32,32,768]{2,1,0:T(8,128)} custom-call(f32[1,2048]{1,0:T(1,128)} %get-tuple-element.5.flux_v, s32[1,2048]{1,0:T(1,128)} %cell_v.3, f32[32,32,768]{2,1,0:T(8,128)} %get-tuple-element.6.adv), custom_call_target="tpu_custom_call" | custom-call | tf_op jit(solution)/shard_map/sink/pallas_call | solution.py:498
  63.2 0.0 copy-done
  63.2 0.7 %copy.11 = f32[8,8,768]{2,1,0:T(8,128)} copy(f32[8,8,768]{2,1,0:T(8,128)S(1)} %copy-done) | data formatting | bytes 393216
Async XLA Ops:
  52.6 10.7 %copy-start = (f32[8,8,768]{2,1,0:T(8,128)S(1)}, f32[8,8,768]{2,1,0:T(8,128)}, u32[]{:S(2)}) copy-start(f32[8,8,768]{2,1,0:T(8,128)} %get-tuple-element.13) | copy-start | bytes 589828

commit v2 on v1

v2 whole, which is shorter than its diff:
```python
import jax
import jax.numpy as jnp
from jax import lax
from jax.experimental import pallas as pl
from jax.experimental.pallas import tpu as pltpu
from jax.sharding import PartitionSpec as P

F32 = jnp.float32
BF = jnp.bfloat16
I32 = jnp.int32
MESH = pl.DeviceIdType.MESH

NX, NY, NZ = 32, 32, 768
WX, WY = 8, 8
ZB = NZ // 128
SLOTS = 512
FACES = 2048
GRP, BLK = 8, 16
ROWS = WX * WY * ZB
PACK = 4
SINK = 4
CUTS = (10, 26, 1)


def split3(v):
    hi = v.astype(BF).astype(F32)
    rest = v - hi
    mid = rest.astype(BF).astype(F32)
    return hi, mid, rest - mid


def dot(a, b):
    return lax.dot_general(a, b, (((1,), (0,)), ((), ())), preferred_element_type=F32)


def dot_nt(a, b):
    return lax.dot_general(a, b, (((1,), (1,)), ((), ())), preferred_element_type=F32)


def onehot(index, count):
    rows = lax.broadcasted_iota(I32, (count, index.shape[1]), 0)
    return jnp.where(rows == index, 1.0, 0.0).astype(BF)


def face(a, b, va, vb):
    w = va + vb
    return b * w + (jnp.maximum(w, 0.0) + 0.4) * (a - b)


def shift_up(v, lane):
    r = pltpu.roll(v, 1, 1)
    first = jnp.where(lane == 0, 0.0, r[:, :128])
    return jnp.concatenate([first, r[:, 128:]], axis=1)


def shift_down(v, lane, last):
    r = pltpu.roll(v, v.shape[1] - 1, 1)
    top = jnp.where(lane == 127, last, r[:, -128:])
    return jnp.concatenate([r[:, :-128], top], axis=1)


def sink_weights(flux, cell, weights, rowcode):
    xy = ((cell >> 8) * 43691) >> 17
    zb = (cell >> 7) - 6 * xy
    rowcode[...] = (xy >> 5) * 192 + zb * 32 + (xy & 31)
    mask = lax.broadcasted_iota(I32, (128, FACES), 0) == (cell & 127)
    flux = -0.2 * flux
    hi = flux.astype(BF).astype(F32)
    weights[0:128, :] = jnp.where(mask, hi, 0.0).astype(BF)
    weights[128:256, :] = jnp.where(mask, flux - hi, 0.0).astype(BF)


def sink(group, weights, rowcode):
    hot = onehot(rowcode[...] - group * (SINK * 192), SINK * 192)
    total = dot_nt(hot, weights[...])
    return total[:, 0:128] + total[:, 128:256]


def main_kernel(
    cell_v, owner_v, target_v, cond_v, fluid, vel, solid, kond,
    adv_out, solid_out,
    rows_v, rows_s,
    tg, tp, vy, vx, vz, adv, buf, tf_s, rank_s, snd, inc, flx, ret, rmat,
    xrcv, ysnd, yrcv, cur, sysnd, syrcv, kp, inv, base, table, dep, gs, gxs, weights, rowcode,
    lsem, ssem, rsem, osem, isem, fsem, bsem, wsem,
):
    g = lax.axis_index("grp")
    b = lax.axis_index("blk")
    has = {("g", 0): g > 0, ("g", 1): g < GRP - 1, ("b", 0): b > 0, ("b", 1): b < BLK - 1}

    def neighbour(axis, side):
        step = 1 if side else -1
        return (g + step, b) if axis == "g" else (g, b + step)

    cell = cell_v[...]
    cell_xy = ((cell >> 8) * 43691) >> 17
    rows_v[...] = ((cell >> 7) - 6 * cell_xy) * (NX * NY) + cell_xy
    rows_copy = pltpu.make_async_copy(rows_v, rows_s, lsem.at[12])
    rows_copy.start()
    loads = []

    def load(src, dst):
        c = pltpu.make_async_copy(src, dst, lsem.at[len(loads)])
        c.start()
        loads.append(c)

    for zb in range(ZB):
        load(fluid.at[:, :, pl.ds(zb * 128, 128)], tg.at[zb])
    load(solid, cur.at[0, pl.ds(1, WX), pl.ds(8, WY), :])
    load(fluid, tp)
    load(vel.at[1], vy)
    load(vel.at[0], vx)
    load(vel.at[2], vz)
    load(kond, kp)

    bar = pltpu.get_barrier_semaphore()

    def greet(k, carry):
        pl.semaphore_signal(bar, inc=1, device_id=(g, lax.rem(b + k, BLK)), device_id_type=MESH)
        return carry

    lax.fori_loop(1, BLK, greet, 0)
    for side in (0, 1):
        @pl.when(has["g", side])
        def _():
            pl.semaphore_signal(bar, inc=1, device_id=neighbour("g", side), device_id_type=MESH)

    for side in (0, 1):
        @pl.when(jnp.logical_not(has["g", side]))
        def _():
            xrcv[side] = jnp.zeros((2, NY, NZ), F32)
            wat = 0 if side == 0 else WX + 1
            for k in range(4):
                cur[k, wat, 8:16, :] = jnp.zeros((WY, NZ), F32)

        @pl.when(jnp.logical_not(has["b", side]))
        def _():
            yrcv[side] = jnp.zeros((2, NX, NZ), F32)
            for k in range(4):
                syrcv[k, side] = jnp.zeros((WX, NZ), F32)

    owner = owner_v[...]
    own16 = onehot(owner, BLK)
    upper = jnp.where(
        lax.broadcasted_iota(I32, (128, 128), 0) <= lax.broadcasted_iota(I32, (128, 128), 1), 1.0, 0.0
    ).astype(BF)
    offset = jnp.zeros((BLK, 1), F32)
    for c in range(FACES // 128):
        mine = own16[:, c * 128:(c + 1) * 128]
        running = dot(mine, upper) + offset
        offset = running[:, 127:128]
        rank_s[:, c * 128:(c + 1) * 128] = (
            jnp.sum(jnp.where(mine.astype(F32) > 0.5, running, 0.0), axis=0, keepdims=True) - 1.0
        ).astype(I32)

    def remote(src, dst, at, device):
        return pltpu.make_async_remote_copy(
            src_ref=src, dst_ref=dst, send_sem=ssem.at[at], recv_sem=rsem.at[at],
            device_id=device, device_id_type=MESH,
        )

    def message(kind, axis, k=0):
        out = []
        for slot in (0, 1):
            side = 1 - slot
            to = neighbour(axis, side)
            if kind == "t":
                c = remote(fluid.at[NX - 1 if side else 0],
                           xrcv.at[slot, 0], slot, to)
            elif kind == "v":
                c = remote(vel.at[0, NX - 1 if side else 0], xrcv.at[slot, 1], 2 + slot, to)
            elif kind == "y":
                c = remote(ysnd.at[side], yrcv.at[slot], 4 + slot, to)
            elif kind == "sx":
                c = remote(cur.at[k, WX if side else 1, pl.ds(8, WY), :],
                           cur.at[k, WX + 1 if slot else 0, pl.ds(8, WY), :], 6 + 2 * k + slot, to)
            else:
                c = remote(sysnd.at[k, side], syrcv.at[k, slot], 14 + 2 * k + slot, to)
            out.append(c)
        return out

    def send(kind, axis, k=0):
        for slot, c in enumerate(message(kind, axis, k)):
            @pl.when(has[axis, 1 - slot])
            def _():
                c.start()

    def receive(kind, axis, k=0):
        for slot, c in enumerate(message(kind, axis, k)):
            @pl.when(has[axis, slot])
            def _():
                c.wait_recv()

    def sent(kind, axis, k=0):
        for slot, c in enumerate(message(kind, axis, k)):
            @pl.when(has[axis, 1 - slot])
            def _():
                c.wait_send()

    def solid_send(k):
        for x in range(WX):
            sysnd[k, 0, x:x + 1, :] = cur[k, x + 1, 8:9, :]
            sysnd[k, 1, x:x + 1, :] = cur[k, x + 1, 15:16, :]
        send("sx", "g", k)
        send("sy", "b", k)

    def solid_receive(k):
        receive("sx", "g", k)
        receive("sy", "b", k)
        for x in range(WX):
            cur[k, x + 1, 7:8, :] = syrcv[k, 0, x:x + 1, :]
            cur[k, x + 1, 16:17, :] = syrcv[k, 1, x:x + 1, :]

    for i in range(ZB):
        loads[i].wait()
    rows_copy.wait()
    flat = tg.reshape(ZB * NX * NY, 128)

    def gather(i, carry):
        at = pl.multiple_of(i * 16, 16)
        for u in range(16):
            buf[pl.ds(at + u, 1), :] = flat[pl.ds(rows_s[0, at + u], 1), :]
        return carry

    lax.fori_loop(0, FACES // 16, gather, 0)
    lane128 = lax.broadcasted_iota(I32, (128, 128), 0)
    for c in range(FACES // 128):
        cols = slice(c * 128, (c + 1) * 128)
        block = buf[cols, :].T
        lane = cell_v[:, cols] & 127
        tf_s[:, cols] = jnp.sum(jnp.where(lane128 == lane, block, 0.0), axis=0, keepdims=True)

    target = target_v[...]
    target_xy = ((target >> 8) * 43691) >> 17
    code = (((target >> 7) - 6 * target_xy) * (WX * WY) + target_xy) * 128 + (target & 127)
    mine = lax.broadcasted_iota(I32, (BLK, FACES), 0) == owner
    fields = list(split3(tf_s[...])) + list(split3(cond_v[...]))
    fields += [((code >> 8) << 8).astype(F32), (code & 255).astype(F32)]
    many = jnp.concatenate([jnp.where(mine, f, 0.0).astype(BF) for f in fields], axis=0)
    placed = dot_nt(many, onehot(rank_s[...], SLOTS))
    for i, (lo, hi) in enumerate(((0, 3), (3, 6), (6, 8))):
        part = placed[lo * BLK:(lo + 1) * BLK]
        for f in range(lo + 1, hi):
            part = part + placed[f * BLK:(f + 1) * BLK]
        for j in range(BLK):
            snd[j, :, i * SLOTS:(i + 1) * SLOTS] = part[j:j + 1, :]

    def row_copy(k):
        to = lax.rem(b + k, BLK)
        return pltpu.make_async_remote_copy(
            src_ref=snd.at[to], dst_ref=inc.at[b],
            send_sem=osem.at[k], recv_sem=isem.at[k], device_id=(g, to), device_id_type=MESH)

    def flux_copy(k):
        to = lax.rem(b + BLK - k, BLK)
        return pltpu.make_async_remote_copy(
            src_ref=flx.at[to], dst_ref=ret.at[b],
            send_sem=fsem.at[k], recv_sem=bsem.at[k], device_id=(g, to), device_id_type=MESH)

    def row_send(k, carry):
        row_copy(k).start()
        return carry

    greeted = 15 + has["g", 0].astype(I32) + has["g", 1].astype(I32)
    pl.semaphore_wait(bar, greeted)
    lax.fori_loop(1, BLK, row_send, 0)

    loads[6].wait()
    solid_send(0)
    for i in (7, 8):
        loads[i].wait()

    def pack(x, carry):
        ysnd[0, 0, pl.ds(x, 1), :] = tp[x, 0:1, :]
        ysnd[1, 0, pl.ds(x, 1), :] = tp[x, NY - 1:NY, :]
        ysnd[0, 1, pl.ds(x, 1), :] = vy[x, 0:1, :]
        ysnd[1, 1, pl.ds(x, 1), :] = vy[x, NY - 1:NY, :]
        return carry

    lax.fori_loop(0, NX, pack, 0)
    send("y", "b")
    send("t", "g")
    send("v", "g")

    lane = lax.broadcasted_iota(I32, (8, 128), 1)
    loads[11].wait()
    for x in range(WX):
        k0, k1, k2 = kp[0, x], kp[1, x], kp[2, x]
        r = 1.0 / (0.5 + 2.0 * (k0 + k1 + k2))
        inv[x] = r
        kp[0, x] = k0 * r
        kp[1, x] = k1 * r
        kp[2, x] = k2 * r
    for zb in range(ZB):
        for x in range(WX):
            at = zb * 64 + x * 8
            dep[at:at + 8, 0:128] = cur[0, x + 1, 8:16, zb * 128:(zb + 1) * 128]
    across = dep[:, 0:128].T
    for i, part in enumerate(split3(across)):
        table[i * 128:(i + 1) * 128, :] = part.astype(BF)
    dep[...] = jnp.zeros((ROWS, 256), F32)

    loads[9].wait()
    loads[10].wait()
    gxs[...] = jnp.zeros((NY, NZ), F32)
    sub = lax.broadcasted_iota(I32, (8, NZ), 0)

    def slab(x, carry, end=False):
        def finish(t, lower, upper):
            r = 8 * t
            here = tp[x, r:r + 8, :]
            total = gxs[r:r + 8, :] + (lower - upper)
            if not end:
                high = face(here, tp[x + 1, r:r + 8, :], vx[x, r:r + 8, :], vx[x + 1, r:r + 8, :])
                total = total - high
                gxs[r:r + 8, :] = high
            v = vz[x, r:r + 8, :]
            bottom = face(shift_up(here, lane), here, shift_up(v, lane), v)
            last = face(here[:, -128:], 0.0, v[:, -128:], 0.0)
            top = shift_down(bottom, lane, last)
            adv[x, r:r + 8, :] = here + 0.1 * (total + (bottom - top))

        zero = jnp.zeros((8, NZ), F32)
        temp0 = vel0 = low = low_up = zero
        for t in range(4):
            r = 8 * t
            here, v = tp[x, r:r + 8, :], vy[x, r:r + 8, :]
            temp1, vel1 = pltpu.roll(here, 1, 0), pltpu.roll(v, 1, 0)
            g_t = face(jnp.where(sub == 0, temp0, temp1), here, jnp.where(sub == 0, vel0, vel1), v)
            if t == 0:
                g_t = jnp.where(sub == 0, 0.0, g_t)
            g_up = pltpu.roll(g_t, 7, 0)
            if t > 0:
                finish(t - 1, low, jnp.where(sub == 7, g_up, low_up))
            temp0, vel0, low, low_up = temp1, vel1, g_t, g_up
        finish(3, low, jnp.where(sub == 7, 0.0, low_up))
        return carry

    lax.fori_loop(0, CUTS[0], slab, 0)

    own_at = pl.ds(b, 1)
    inc[own_at] = snd[own_at]

    def owned(q, carry):
        for j in range(PACK):
            @pl.when(q * PACK + j > 0)
            def _():
                row_copy(q * PACK + j).wait_recv()

        src = [lax.rem(b + BLK - q * PACK - j, BLK) for j in range(PACK)]
        field = [jnp.concatenate([inc[i][:, f * SLOTS:(f + 1) * SLOTS] for i in src], axis=1) for f in range(3)]
        code = field[2].astype(I32)
        hot = onehot(code >> 7, ROWS)
        mask = lax.broadcasted_iota(I32, (128, PACK * SLOTS), 0) == (code & 127)
        found = dot(table[...], hot)
        found = found[0:128] + found[128:256] + found[256:384]
        wall = jnp.sum(jnp.where(mask, found, 0.0), axis=0, keepdims=True)
        flux = field[1] * (field[0] - wall)
        hi = flux.astype(BF).astype(F32)
        spread = jnp.concatenate([jnp.where(mask, hi, 0.0), jnp.where(mask, flux - hi, 0.0)], axis=0)
        for j, i in enumerate(src):
            flx[i] = flux[:, j * SLOTS:(j + 1) * SLOTS]
        dep[...] += dot_nt(hot, spread.astype(BF))
        for j in range(PACK):
            @pl.when(q * PACK + j > 0)
            def _():
                flux_copy(q * PACK + j).start()

        return carry

    lax.fori_loop(0, BLK // PACK, owned, 0)

    def sweep(k, x):
        here = cur[k, x + 1, 8:16, :]
        beside = kp[0, x] * (cur[k, x + 2, 8:16, :] + cur[k, x, 8:16, :])
        beside = beside + kp[1, x] * (cur[k, x + 1, 9:17, :] + cur[k, x + 1, 7:15, :])
        beside = beside + kp[2, x] * (shift_up(here, lane) + shift_down(here, lane, 0.0))
        return base[x] + beside

    solid_receive(0)
    for x in range(WX):
        deposit = jnp.concatenate(
            [dep[zb * 64 + x * 8:zb * 64 + x * 8 + 8, 0:128] + dep[zb * 64 + x * 8:zb * 64 + x * 8 + 8, 128:256]
             for zb in range(ZB)], axis=1)
        base[x] = (0.5 * cur[0, x + 1, 8:16, :] + deposit) * inv[x]
        cur[1, x + 1, 8:16, :] = sweep(0, x)
    solid_send(1)
    lax.fori_loop(CUTS[0], CUTS[1], slab, 0)
    solid_receive(1)
    for x in range(WX):
        cur[2, x + 1, 8:16, :] = sweep(1, x)
    solid_send(2)
    lax.fori_loop(CUTS[1], NX - 1, slab, 0)
    slab(NX - 1, 0, True)

    ret[own_at] = flx[own_at]

    def returned(k, carry):
        flux_copy(k).wait_recv()
        return carry

    lax.fori_loop(1, BLK, returned, 0)
    for j in range(BLK):
        rmat[j:j + 1, :] = ret[j]
    stacked = jnp.concatenate(list(split3(rmat[...])), axis=0).astype(BF)
    back = dot(stacked, onehot(rank_s[...], SLOTS))
    back = back[0:16] + back[16:32] + back[32:48]
    flux = jnp.sum(jnp.where(mine, back, 0.0), axis=0, keepdims=True)
    sink_weights(flux, cell_v[...], weights, rowcode)

    receive("y", "b")
    gs[...] = 0.1 * face(yrcv[0, 0], ysnd[0, 0], yrcv[0, 1], ysnd[0, 1])
    gxs[...] = 0.1 * face(ysnd[1, 0], yrcv[1, 0], ysnd[1, 1], yrcv[1, 1])

    def edge(x, carry):
        adv[x, 0:1, :] += gs[pl.ds(x, 1), :]
        adv[x, NY - 1:NY, :] -= gxs[pl.ds(x, 1), :]
        return carry

    lax.fori_loop(0, NX, edge, 0)
    receive("t", "g")
    receive("v", "g")
    adv[0] += 0.1 * face(xrcv[0, 0], tp[0], xrcv[0, 1], vx[0])
    adv[NX - 1] -= 0.1 * face(tp[NX - 1], xrcv[1, 0], vx[NX - 1], xrcv[1, 1])

    def result(i):
        at = pl.ds(i * SINK, SINK)
        return pltpu.make_async_copy(adv.at[at], adv_out.at[at], wsem.at[i])

    def sink_group(i, carry):
        total = sink(i, weights, rowcode)
        for x in range(SINK):
            for zb in range(ZB):
                at = x * 192 + zb * 32
                cols = slice(zb * 128, (zb + 1) * 128)
                adv[i * SINK + x, :, cols] += total[at:at + 32, :]
        result(i).start()
        return carry

    lax.fori_loop(0, CUTS[2], sink_group, 0)
    solid_receive(2)
    for x in range(WX):
        cur[3, x + 1, 8:16, :] = sweep(2, x)
    solid_send(3)
    lax.fori_loop(CUTS[2], NX // SINK, sink_group, 0)
    solid_receive(3)
    for x in range(WX):
        solid_out[x] = sweep(3, x)

    def drained(k, carry):
        row_copy(k).wait_send()
        flux_copy(k).wait_send()
        return carry

    lax.fori_loop(1, BLK, drained, 0)
    sent("t", "g")
    sent("v", "g")
    sent("y", "b")
    for k in range(4):
        sent("sx", "g", k)
        sent("sy", "b", k)
    for i in range(NX // SINK):
        result(i).wait()


def shards(fluid, vel, solid, kond, cell, owner, target, cond):
    vmem = pl.BlockSpec(memory_space=pltpu.VMEM)
    any_ = pl.BlockSpec(memory_space=pl.ANY)
    dma = pltpu.SemaphoreType.DMA
    return pl.pallas_call(
        main_kernel,
        out_shape=(
            jax.ShapeDtypeStruct((NX, NY, NZ), F32),
            jax.ShapeDtypeStruct((WX, WY, NZ), F32),
        ),
        in_specs=[vmem] * 4 + [any_] * 4,
        out_specs=(any_, vmem),
        scratch_shapes=[
            pltpu.VMEM((1, FACES), I32),
            pltpu.SMEM((1, FACES), I32),
            pltpu.VMEM((ZB, NX, NY, 128), F32),
            pltpu.VMEM((NX, NY, NZ), F32),
            pltpu.VMEM((NX, NY, NZ), F32),
            pltpu.VMEM((NX, NY, NZ), F32),
            pltpu.VMEM((NX, NY, NZ), F32),
            pltpu.VMEM((NX, NY, NZ), F32),
            pltpu.VMEM((FACES, 128), F32),
            pltpu.VMEM((1, FACES), F32),
            pltpu.VMEM((1, FACES), I32),
            pltpu.VMEM((BLK, 1, 3 * SLOTS), F32),
            pltpu.VMEM((BLK, 1, 3 * SLOTS), F32),
            pltpu.VMEM((BLK, 1, SLOTS), F32),
            pltpu.VMEM((BLK, 1, SLOTS), F32),
            pltpu.VMEM((BLK, SLOTS), F32),
            pltpu.VMEM((2, 2, NY, NZ), F32),
            pltpu.VMEM((2, 2, NX, NZ), F32),
            pltpu.VMEM((2, 2, NX, NZ), F32),
            pltpu.VMEM((4, WX + 2, 24, NZ), F32),
            pltpu.VMEM((4, 2, WX, NZ), F32),
            pltpu.VMEM((4, 2, WX, NZ), F32),
            pltpu.VMEM((3, WX, WY, NZ), F32),
            pltpu.VMEM((WX, WY, NZ), F32),
            pltpu.VMEM((WX, WY, NZ), F32),
            pltpu.VMEM((3 * 128, ROWS), BF),
            pltpu.VMEM((ROWS, 256), F32),
            pltpu.VMEM((NX, NZ), F32),
            pltpu.VMEM((NY, NZ), F32),
            pltpu.VMEM((256, FACES), BF),
            pltpu.VMEM((1, FACES), I32),
            dma((13,)), dma((22,)), dma((22,)), dma((BLK,)), dma((BLK,)), dma((BLK,)), dma((BLK,)), dma((NX // SINK,)),
        ],
        compiler_params=pltpu.CompilerParams(
            collective_id=0, has_side_effects=True, vmem_limit_bytes=60 * 1024 * 1024),
        name="exchange",
    )(cell, owner, target, cond, fluid, vel, solid, kond)


def solution(mesh):
    in_specs = (
        P("grp", "blk", None),
        P(None, "grp", "blk", None),
        P("grp", "blk", None),
        P(None, "grp", "blk", None),
        P("grp", "blk"),
        P("grp", "blk"),
        P("grp", "blk"),
        P("grp", "blk"),
    )
    out_specs = (P("grp", "blk", None), P("grp", "blk", None))
    return jax.shard_map(shards, mesh=mesh, in_specs=in_specs, out_specs=out_specs, check_vma=False)
```

time: 64.4 us -> 48.1 us (0.75)
  the two profiles are of different devices: /device:TPU:14 before, /device:TPU:6 now
where the time goes in v2:
time: 48.1 us; the launch traced here: 47.9 us
  Pallas kernels  42.7 us (89%)
  local copies, waits for them, and re-layouts  4.62 us (10%)
  between operations  0.65 us (1%)
    pallas_call x1, Pallas kernels, shards(): pl.pallas_call(main_kernel, out_shape=(jax.ShapeDtypeStruct((NX, NY, NZ),...  42.7 us
    unnamed x4, local copies, waits for them, and re-layouts  4.62 us

profile of v2, /device:TPU:6, one launch (start us, length us, event | category | flops | bytes accessed | tf_op | source)
XLA Modules:
  0.0 47.9 jit_solution(8927542977778037326)
XLA Ops:
  0.6 42.7 %exchange.1 = (f32[32,32,768]{2,1,0:T(8,128)}, f32[8,8,768]{2,1,0:T(8,128)}) custom-call(s32[1,2048]{1,0:T(1,128)} %cell_v.1, s32[1,2048]{1,0:T(1,128)} %owner_v.1, s32[1,2048]{1,0:T(1,128)} %target_v.1, f32[1,2048]{1,0:T(1,128)} %cond_v.1, f32[32,32,768]{2,1,0:T(8,128)} %fluid.1, f32[3,32,32,768]{3,2,1,0:T(8,128)} %vel.1, f32[8,8,768]{2,1,0:T(8,128)} %solid.1, ...), custom_call_target="tpu_custom_call" | custom-call | tf_op jit(solution)/shard_map/exchange/pallas_call | solution.py:470
  43.3 0.0 copy-start
  43.3 3.9 %copy.12 = f32[32,32,768]{2,1,0:T(8,128)} copy(f32[32,32,768]{2,1,0:T(8,128)} %get-tuple-element.4) | data formatting | bytes 6291456
  47.3 0.0 copy-done
  47.3 0.7 %copy.13 = f32[8,8,768]{2,1,0:T(8,128)} copy(f32[8,8,768]{2,1,0:T(8,128)S(1)} %copy-done) | data formatting | bytes 393216
Async XLA Ops:
  43.3 4.0 %copy-start = (f32[8,8,768]{2,1,0:T(8,128)S(1)}, f32[8,8,768]{2,1,0:T(8,128)}, u32[]{:S(2)}) copy-start(f32[8,8,768]{2,1,0:T(8,128)} %get-tuple-element.5) | copy-start | bytes 589828

commit v3 on v2

--- a/solution.py
+++ b/solution.py
@@ -19,7 +19,7 @@
 ROWS = WX * WY * ZB
 PACK = 4
 SINK = 4
-CUTS = (10, 26, 1)
+CUTS = (15, 0, 3)
 
 
 def split3(v):
@@ -78,11 +78,11 @@
 
 def main_kernel(
     cell_v, owner_v, target_v, cond_v, fluid, vel, solid, kond,
-    adv_out, solid_out,
+    adv, solid_out,
     rows_v, rows_s,
-    tg, tp, vy, vx, vz, adv, buf, tf_s, rank_s, snd, inc, flx, ret, rmat,
+    tg, vy, vx, vz, buf, tf_s, rank_s, snd, inc, flx, ret, rmat,
     xrcv, ysnd, yrcv, cur, sysnd, syrcv, kp, inv, base, table, dep, gs, gxs, weights, rowcode,
-    lsem, ssem, rsem, osem, isem, fsem, bsem, wsem,
+    lsem, ssem, rsem, osem, isem, fsem, bsem,
 ):
     g = lax.axis_index("grp")
     b = lax.axis_index("blk")
@@ -95,7 +95,7 @@
     cell = cell_v[...]
     cell_xy = ((cell >> 8) * 43691) >> 17
     rows_v[...] = ((cell >> 7) - 6 * cell_xy) * (NX * NY) + cell_xy
-    rows_copy = pltpu.make_async_copy(rows_v, rows_s, lsem.at[12])
+    rows_copy = pltpu.make_async_copy(rows_v, rows_s, lsem.at[14])
     rows_copy.start()
     loads = []
 
@@ -104,14 +104,18 @@
         c.start()
         loads.append(c)
 
+    load(solid, cur.at[0, pl.ds(1, WX), pl.ds(8, WY), :])
     for zb in range(ZB):
         load(fluid.at[:, :, pl.ds(zb * 128, 128)], tg.at[zb])
-    load(solid, cur.at[0, pl.ds(1, WX), pl.ds(8, WY), :])
-    load(fluid, tp)
     load(vel.at[1], vy)
-    load(vel.at[0], vx)
-    load(vel.at[2], vz)
+    load(vel.at[0, pl.ds(0, 9)], vx.at[pl.ds(0, 9)])
+    load(vel.at[2, pl.ds(0, 8)], vz.at[pl.ds(0, 8)])
+    load(vel.at[0, pl.ds(9, NX - 9)], vx.at[pl.ds(9, NX - 9)])
+    load(vel.at[2, pl.ds(8, NX - 8)], vz.at[pl.ds(8, NX - 8)])
     load(kond, kp)
+
+    def temp(x, rows):
+        return jnp.concatenate([tg[zb, x, rows, :] for zb in range(ZB)], axis=1)
 
     bar = pltpu.get_barrier_semaphore()
 
@@ -144,14 +148,15 @@
     upper = jnp.where(
         lax.broadcasted_iota(I32, (128, 128), 0) <= lax.broadcasted_iota(I32, (128, 128), 1), 1.0, 0.0
     ).astype(BF)
-    offset = jnp.zeros((BLK, 1), F32)
+    inside = dot(jnp.concatenate([own16[:, c * 128:(c + 1) * 128] for c in range(FACES // 128)], axis=0), upper)
+    mine = lax.broadcasted_iota(I32, (BLK, FACES), 0) == owner
+    offset = jnp.full((BLK, 1), -1.0, F32)
     for c in range(FACES // 128):
-        mine = own16[:, c * 128:(c + 1) * 128]
-        running = dot(mine, upper) + offset
-        offset = running[:, 127:128]
-        rank_s[:, c * 128:(c + 1) * 128] = (
-            jnp.sum(jnp.where(mine.astype(F32) > 0.5, running, 0.0), axis=0, keepdims=True) - 1.0
-        ).astype(I32)
+        cols = slice(c * 128, (c + 1) * 128)
+        running = inside[c * BLK:(c + 1) * BLK]
+        rank_s[:, cols] = jnp.sum(
+            jnp.where(mine[:, cols], running + offset, 0.0), axis=0, keepdims=True).astype(I32)
+        offset = offset + running[:, 127:128]
 
     def remote(src, dst, at, device):
         return pltpu.make_async_remote_copy(
@@ -211,18 +216,18 @@
             cur[k, x + 1, 7:8, :] = syrcv[k, 0, x:x + 1, :]
             cur[k, x + 1, 16:17, :] = syrcv[k, 1, x:x + 1, :]
 
-    for i in range(ZB):
+    for i in range(1, 7):
         loads[i].wait()
     rows_copy.wait()
     flat = tg.reshape(ZB * NX * NY, 128)
 
     def gather(i, carry):
-        at = pl.multiple_of(i * 16, 16)
-        for u in range(16):
+        at = pl.multiple_of(i * 64, 64)
+        for u in range(64):
             buf[pl.ds(at + u, 1), :] = flat[pl.ds(rows_s[0, at + u], 1), :]
         return carry
 
-    lax.fori_loop(0, FACES // 16, gather, 0)
+    lax.fori_loop(0, FACES // 64, gather, 0)
     lane128 = lax.broadcasted_iota(I32, (128, 128), 0)
     for c in range(FACES // 128):
         cols = slice(c * 128, (c + 1) * 128)
@@ -233,7 +238,6 @@
     target = target_v[...]
     target_xy = ((target >> 8) * 43691) >> 17
     code = (((target >> 7) - 6 * target_xy) * (WX * WY) + target_xy) * 128 + (target & 127)
-    mine = lax.broadcasted_iota(I32, (BLK, FACES), 0) == owner
     fields = list(split3(tf_s[...])) + list(split3(cond_v[...]))
     fields += [((code >> 8) << 8).astype(F32), (code & 255).astype(F32)]
     many = jnp.concatenate([jnp.where(mine, f, 0.0).astype(BF) for f in fields], axis=0)
@@ -265,16 +269,15 @@
     pl.semaphore_wait(bar, greeted)
     lax.fori_loop(1, BLK, row_send, 0)
 
-    loads[6].wait()
+    loads[0].wait()
     solid_send(0)
-    for i in (7, 8):
-        loads[i].wait()
+    loads[7].wait()
+    lane = lax.broadcasted_iota(I32, (8, 128), 1)
 
     def pack(x, carry):
-        ysnd[0, 0, pl.ds(x, 1), :] = tp[x, 0:1, :]
-        ysnd[1, 0, pl.ds(x, 1), :] = tp[x, NY - 1:NY, :]
-        ysnd[0, 1, pl.ds(x, 1), :] = vy[x, 0:1, :]
-        ysnd[1, 1, pl.ds(x, 1), :] = vy[x, NY - 1:NY, :]
+        for side, rows in ((0, slice(0, 1)), (1, slice(NY - 1, NY))):
+            ysnd[side, 0, pl.ds(x, 1), :] = temp(x, rows)
+            ysnd[side, 1, pl.ds(x, 1), :] = vy[x, rows, :]
         return carry
 
     lax.fori_loop(0, NX, pack, 0)
@@ -282,8 +285,7 @@
     send("t", "g")
     send("v", "g")
 
-    lane = lax.broadcasted_iota(I32, (8, 128), 1)
-    loads[11].wait()
+    loads[12].wait()
     for x in range(WX):
         k0, k1, k2 = kp[0, x], kp[1, x], kp[2, x]
         r = 1.0 / (0.5 + 2.0 * (k0 + k1 + k2))
@@ -300,18 +302,18 @@
         table[i * 128:(i + 1) * 128, :] = part.astype(BF)
     dep[...] = jnp.zeros((ROWS, 256), F32)
 
-    loads[9].wait()
-    loads[10].wait()
+    for i in range(8, 12):
+        loads[i].wait()
     gxs[...] = jnp.zeros((NY, NZ), F32)
     sub = lax.broadcasted_iota(I32, (8, NZ), 0)
 
     def slab(x, carry, end=False):
         def finish(t, lower, upper):
             r = 8 * t
-            here = tp[x, r:r + 8, :]
+            here = temp(x, slice(r, r + 8))
             total = gxs[r:r + 8, :] + (lower - upper)
             if not end:
-                high = face(here, tp[x + 1, r:r + 8, :], vx[x, r:r + 8, :], vx[x + 1, r:r + 8, :])
+                high = face(here, temp(x + 1, slice(r, r + 8)), vx[x, r:r + 8, :], vx[x + 1, r:r + 8, :])
                 total = total - high
                 gxs[r:r + 8, :] = high
             v = vz[x, r:r + 8, :]
@@ -324,7 +326,7 @@
         temp0 = vel0 = low = low_up = zero
         for t in range(4):
             r = 8 * t
-            here, v = tp[x, r:r + 8, :], vy[x, r:r + 8, :]
+            here, v = temp(x, slice(r, r + 8)), vy[x, r:r + 8, :]
             temp1, vel1 = pltpu.roll(here, 1, 0), pltpu.roll(v, 1, 0)
             g_t = face(jnp.where(sub == 0, temp0, temp1), here, jnp.where(sub == 0, vel0, vel1), v)
             if t == 0:
@@ -385,14 +387,12 @@
         base[x] = (0.5 * cur[0, x + 1, 8:16, :] + deposit) * inv[x]
         cur[1, x + 1, 8:16, :] = sweep(0, x)
     solid_send(1)
-    lax.fori_loop(CUTS[0], CUTS[1], slab, 0)
+    lax.fori_loop(CUTS[0], NX - 1, slab, 0)
+    slab(NX - 1, 0, True)
     solid_receive(1)
     for x in range(WX):
         cur[2, x + 1, 8:16, :] = sweep(1, x)
     solid_send(2)
-    lax.fori_loop(CUTS[1], NX - 1, slab, 0)
-    slab(NX - 1, 0, True)
-
     ret[own_at] = flx[own_at]
 
     def returned(k, carry):
@@ -420,12 +420,8 @@
     lax.fori_loop(0, NX, edge, 0)
     receive("t", "g")
     receive("v", "g")
-    adv[0] += 0.1 * face(xrcv[0, 0], tp[0], xrcv[0, 1], vx[0])
-    adv[NX - 1] -= 0.1 * face(tp[NX - 1], xrcv[1, 0], vx[NX - 1], xrcv[1, 1])
-
-    def result(i):
-        at = pl.ds(i * SINK, SINK)
-        return pltpu.make_async_copy(adv.at[at], adv_out.at[at], wsem.at[i])
+    adv[0] += 0.1 * face(xrcv[0, 0], temp(0, slice(0, NY)), xrcv[0, 1], vx[0])
+    adv[NX - 1] -= 0.1 * face(temp(NX - 1, slice(0, NY)), xrcv[1, 0], vx[NX - 1], xrcv[1, 1])
 
     def sink_group(i, carry):
         total = sink(i, weights, rowcode)
@@ -434,7 +430,6 @@
                 at = x * 192 + zb * 32
                 cols = slice(zb * 128, (zb + 1) * 128)
                 adv[i * SINK + x, :, cols] += total[at:at + 32, :]
-        result(i).start()
         return carry
 
     lax.fori_loop(0, CUTS[2], sink_group, 0)
@@ -459,28 +454,24 @@
     for k in range(4):
         sent("sx", "g", k)
         sent("sy", "b", k)
-    for i in range(NX // SINK):
-        result(i).wait()
 
 
 def shards(fluid, vel, solid, kond, cell, owner, target, cond):
     vmem = pl.BlockSpec(memory_space=pltpu.VMEM)
-    any_ = pl.BlockSpec(memory_space=pl.ANY)
+    hbm = pl.BlockSpec(memory_space=pltpu.HBM)
     dma = pltpu.SemaphoreType.DMA
     return pl.pallas_call(
         main_kernel,
         out_shape=(
-            jax.ShapeDtypeStruct((NX, NY, NZ), F32),
-            jax.ShapeDtypeStruct((WX, WY, NZ), F32),
+            pltpu.VMEM((NX, NY, NZ), F32),
+            pltpu.VMEM((WX, WY, NZ), F32),
         ),
-        in_specs=[vmem] * 4 + [any_] * 4,
-        out_specs=(any_, vmem),
+        in_specs=[vmem] * 4 + [hbm] * 4,
+        out_specs=(vmem, vmem),
         scratch_shapes=[
             pltpu.VMEM((1, FACES), I32),
             pltpu.SMEM((1, FACES), I32),
             pltpu.VMEM((ZB, NX, NY, 128), F32),
-            pltpu.VMEM((NX, NY, NZ), F32),
-            pltpu.VMEM((NX, NY, NZ), F32),
             pltpu.VMEM((NX, NY, NZ), F32),
             pltpu.VMEM((NX, NY, NZ), F32),
             pltpu.VMEM((NX, NY, NZ), F32),
@@ -507,7 +498,7 @@
             pltpu.VMEM((NY, NZ), F32),
             pltpu.VMEM((256, FACES), BF),
             pltpu.VMEM((1, FACES), I32),
-            dma((13,)), dma((22,)), dma((22,)), dma((BLK,)), dma((BLK,)), dma((BLK,)), dma((BLK,)), dma((NX // SINK,)),
+            dma((15,)), dma((22,)), dma((22,)), dma((BLK,)), dma((BLK,)), dma((BLK,)), dma((BLK,)),
         ],
         compiler_params=pltpu.CompilerParams(
             collective_id=0, has_side_effects=True, vmem_limit_bytes=60 * 1024 * 1024),

time: 48.1 us -> 43.1 us (0.90)
  Pallas kernels: 42.7 us -> 39.9 us
  local copies, waits for them, and re-layouts: 4.62 us -> 2.34 us
    pallas_call x1, Pallas kernels: 42.7 us -> 39.9 us  [shards(): pl.pallas_call(main_kernel, out_shape=(pltpu.VMEM((NX, NY, NZ), F32), plt...]
    unnamed x4 -> x2, local copies, waits for them, and re-layouts: 4.62 us -> 2.34 us
where the time goes in v3:
time: 43.1 us; the launch traced here: 42.9 us
  Pallas kernels  39.9 us (93%)
  local copies, waits for them, and re-layouts  2.34 us (5%)
  between operations  0.64 us (1%)
    pallas_call x1, Pallas kernels, shards(): pl.pallas_call(main_kernel, out_shape=(pltpu.VMEM((NX, NY, NZ), F32), plt...  39.9 us
    unnamed x2, local copies, waits for them, and re-layouts  2.34 us

profile of v3, /device:TPU:6, one launch (start us, length us, event | category | flops | bytes accessed | tf_op | source)
XLA Modules:
  0.0 42.9 jit_solution(6436357513428815163)
XLA Ops:
  0.6 39.9 %exchange.1 = (f32[32,32,768]{2,1,0:T(8,128)S(1)}, f32[8,8,768]{2,1,0:T(8,128)S(1)}) custom-call(s32[1,2048]{1,0:T(1,128)} %cell_v.1, s32[1,2048]{1,0:T(1,128)} %owner_v.1, s32[1,2048]{1,0:T(1,128)} %target_v.1, f32[1,2048]{1,0:T(1,128)} %cond_v.1, f32[32,32,768]{2,1,0:T(8,128)} %fluid.1, f32[3,32,32,768]{3,2,1,0:T(8,128)} %vel.1, f32[8,8,768]{2,1,0:T(8,128)} %solid.1, ...), custom_call_target="tpu_custom_call" | custom-call | tf_op jit(solution)/shard_map/exchange/pallas_call | solution.py:463
  40.6 1.7 %copy.12 = f32[32,32,768]{2,1,0:T(8,128)} copy(f32[32,32,768]{2,1,0:T(8,128)S(1)} %get-tuple-element.2) | data formatting | bytes 6291456
  42.3 0.7 %copy.13 = f32[8,8,768]{2,1,0:T(8,128)} copy(f32[8,8,768]{2,1,0:T(8,128)S(1)} %get-tuple-element.3) | data formatting | bytes 393216

commit v4 on v3

--- a/solution.py
+++ b/solution.py
@@ -19,7 +19,7 @@
 ROWS = WX * WY * ZB
 PACK = 4
 SINK = 4
-CUTS = (15, 0, 3)
+CUTS = (24, 0, 3)
 
 
 def split3(v):
@@ -94,7 +94,9 @@
 
     cell = cell_v[...]
     cell_xy = ((cell >> 8) * 43691) >> 17
-    rows_v[...] = ((cell >> 7) - 6 * cell_xy) * (NX * NY) + cell_xy
+    cell_row = ((cell >> 7) - 6 * cell_xy) * (NX * NY) + cell_xy
+    for c in range(FACES // 128):
+        rows_v[c:c + 1, :] = cell_row[:, c * 128:(c + 1) * 128]
     rows_copy = pltpu.make_async_copy(rows_v, rows_s, lsem.at[14])
     rows_copy.start()
     loads = []
@@ -107,12 +109,6 @@
     load(solid, cur.at[0, pl.ds(1, WX), pl.ds(8, WY), :])
     for zb in range(ZB):
         load(fluid.at[:, :, pl.ds(zb * 128, 128)], tg.at[zb])
-    load(vel.at[1], vy)
-    load(vel.at[0, pl.ds(0, 9)], vx.at[pl.ds(0, 9)])
-    load(vel.at[2, pl.ds(0, 8)], vz.at[pl.ds(0, 8)])
-    load(vel.at[0, pl.ds(9, NX - 9)], vx.at[pl.ds(9, NX - 9)])
-    load(vel.at[2, pl.ds(8, NX - 8)], vz.at[pl.ds(8, NX - 8)])
-    load(kond, kp)
 
     def temp(x, rows):
         return jnp.concatenate([tg[zb, x, rows, :] for zb in range(ZB)], axis=1)
@@ -218,16 +214,20 @@
 
     for i in range(1, 7):
         loads[i].wait()
+    load(vel.at[1], vy)
+    load(vel.at[0], vx)
+    load(vel.at[2], vz)
+    load(kond, kp)
     rows_copy.wait()
     flat = tg.reshape(ZB * NX * NY, 128)
 
     def gather(i, carry):
-        at = pl.multiple_of(i * 64, 64)
-        for u in range(64):
-            buf[pl.ds(at + u, 1), :] = flat[pl.ds(rows_s[0, at + u], 1), :]
-        return carry
-
-    lax.fori_loop(0, FACES // 64, gather, 0)
+        at = pl.multiple_of(i * 128, 128)
+        for u in range(128):
+            buf[pl.ds(at + u, 1), :] = flat[pl.ds(rows_s[i, u], 1), :]
+        return carry
+
+    lax.fori_loop(0, FACES // 128, gather, 0)
     lane128 = lax.broadcasted_iota(I32, (128, 128), 0)
     for c in range(FACES // 128):
         cols = slice(c * 128, (c + 1) * 128)
@@ -249,20 +249,18 @@
         for j in range(BLK):
             snd[j, :, i * SLOTS:(i + 1) * SLOTS] = part[j:j + 1, :]
 
-    def row_copy(k):
-        to = lax.rem(b + k, BLK)
+    def row_copy(to, src):
         return pltpu.make_async_remote_copy(
             src_ref=snd.at[to], dst_ref=inc.at[b],
-            send_sem=osem.at[k], recv_sem=isem.at[k], device_id=(g, to), device_id_type=MESH)
-
-    def flux_copy(k):
-        to = lax.rem(b + BLK - k, BLK)
+            send_sem=osem.at[to], recv_sem=isem.at[src], device_id=(g, to), device_id_type=MESH)
+
+    def flux_copy(to, src):
         return pltpu.make_async_remote_copy(
             src_ref=flx.at[to], dst_ref=ret.at[b],
-            send_sem=fsem.at[k], recv_sem=bsem.at[k], device_id=(g, to), device_id_type=MESH)
+            send_sem=fsem.at[to], recv_sem=bsem.at[src], device_id=(g, to), device_id_type=MESH)
 
     def row_send(k, carry):
-        row_copy(k).start()
+        row_copy(lax.rem(b + k, BLK), b).start()
         return carry
 
     greeted = 15 + has["g", 0].astype(I32) + has["g", 1].astype(I32)
@@ -282,10 +280,7 @@
 
     lax.fori_loop(0, NX, pack, 0)
     send("y", "b")
-    send("t", "g")
-    send("v", "g")
-
-    loads[12].wait()
+    loads[10].wait()
     for x in range(WX):
         k0, k1, k2 = kp[0, x], kp[1, x], kp[2, x]
         r = 1.0 / (0.5 + 2.0 * (k0 + k1 + k2))
@@ -302,7 +297,7 @@
         table[i * 128:(i + 1) * 128, :] = part.astype(BF)
     dep[...] = jnp.zeros((ROWS, 256), F32)
 
-    for i in range(8, 12):
+    for i in range(8, 10):
         loads[i].wait()
     gxs[...] = jnp.zeros((NY, NZ), F32)
     sub = lax.broadcasted_iota(I32, (8, NZ), 0)
@@ -338,18 +333,25 @@
         finish(3, low, jnp.where(sub == 7, 0.0, low_up))
         return carry
 
-    lax.fori_loop(0, CUTS[0], slab, 0)
+    def slabs(i, carry):
+        return slab(2 * i + 1, slab(2 * i, carry))
+
+    lax.fori_loop(0, 6, slabs, 0)
+    send("t", "g")
+    send("v", "g")
+
+    lax.fori_loop(6, CUTS[0] // 2, slabs, 0)
 
     own_at = pl.ds(b, 1)
     inc[own_at] = snd[own_at]
 
     def owned(q, carry):
-        for j in range(PACK):
-            @pl.when(q * PACK + j > 0)
+        src = [(j >> 1) * 8 + q * 2 + (j & 1) for j in range(PACK)]
+        for i in src:
+            @pl.when(i != b)
             def _():
-                row_copy(q * PACK + j).wait_recv()
-
-        src = [lax.rem(b + BLK - q * PACK - j, BLK) for j in range(PACK)]
+                row_copy(i, i).wait_recv()
+
         field = [jnp.concatenate([inc[i][:, f * SLOTS:(f + 1) * SLOTS] for i in src], axis=1) for f in range(3)]
         code = field[2].astype(I32)
         hot = onehot(code >> 7, ROWS)
@@ -363,10 +365,10 @@
         for j, i in enumerate(src):
             flx[i] = flux[:, j * SLOTS:(j + 1) * SLOTS]
         dep[...] += dot_nt(hot, spread.astype(BF))
-        for j in range(PACK):
-            @pl.when(q * PACK + j > 0)
+        for i in src:
+            @pl.when(i != b)
             def _():
-                flux_copy(q * PACK + j).start()
+                flux_copy(i, b).start()
 
         return carry
 
@@ -387,7 +389,8 @@
         base[x] = (0.5 * cur[0, x + 1, 8:16, :] + deposit) * inv[x]
         cur[1, x + 1, 8:16, :] = sweep(0, x)
     solid_send(1)
-    lax.fori_loop(CUTS[0], NX - 1, slab, 0)
+    lax.fori_loop(CUTS[0] // 2, NX // 2 - 1, slabs, 0)
+    slab(NX - 2, 0)
     slab(NX - 1, 0, True)
     solid_receive(1)
     for x in range(WX):
@@ -396,7 +399,8 @@
     ret[own_at] = flx[own_at]
 
     def returned(k, carry):
-        flux_copy(k).wait_recv()
+        other = lax.rem(b + k, BLK)
+        flux_copy(other, other).wait_recv()
         return carry
 
     lax.fori_loop(1, BLK, returned, 0)
@@ -443,8 +447,9 @@
         solid_out[x] = sweep(3, x)
 
     def drained(k, carry):
-        row_copy(k).wait_send()
-        flux_copy(k).wait_send()
+        other = lax.rem(b + k, BLK)
+        row_copy(other, b).wait_send()
+        flux_copy(other, b).wait_send()
         return carry
 
     lax.fori_loop(1, BLK, drained, 0)
@@ -469,8 +474,8 @@
         in_specs=[vmem] * 4 + [hbm] * 4,
         out_specs=(vmem, vmem),
         scratch_shapes=[
-            pltpu.VMEM((1, FACES), I32),
-            pltpu.SMEM((1, FACES), I32),
+            pltpu.VMEM((FACES // 128, 128), I32),
+            pltpu.SMEM((FACES // 128, 128), I32),
             pltpu.VMEM((ZB, NX, NY, 128), F32),
             pltpu.VMEM((NX, NY, NZ), F32),
             pltpu.VMEM((NX, NY, NZ), F32),

time: 43.1 us -> 39.6 us (0.919)
  the two profiles are of different devices: /device:TPU:6 before, /device:TPU:14 now
where the time goes in v4:
time: 39.6 us; the launch traced here: 39.4 us
  Pallas kernels  36.5 us (92%)
  local copies, waits for them, and re-layouts  2.34 us (6%)
  between operations  0.64 us (2%)
    pallas_call x1, Pallas kernels, shards(): pl.pallas_call(main_kernel, out_shape=(pltpu.VMEM((NX, NY, NZ), F32), plt...  36.5 us
    unnamed x2, local copies, waits for them, and re-layouts  2.34 us

profile of v4, /device:TPU:14, one launch (start us, length us, event | category | flops | bytes accessed | tf_op | source)
XLA Modules:
  0.0 39.4 jit_solution(7492152774418323752)
XLA Ops:
  0.6 36.5 %exchange.1 = (f32[32,32,768]{2,1,0:T(8,128)S(1)}, f32[8,8,768]{2,1,0:T(8,128)S(1)}) custom-call(s32[1,2048]{1,0:T(1,128)} %cell_v.1, s32[1,2048]{1,0:T(1,128)} %owner_v.1, s32[1,2048]{1,0:T(1,128)} %target_v.1, f32[1,2048]{1,0:T(1,128)} %cond_v.1, f32[32,32,768]{2,1,0:T(8,128)} %fluid.1, f32[3,32,32,768]{3,2,1,0:T(8,128)} %vel.1, f32[8,8,768]{2,1,0:T(8,128)} %solid.1, ...), custom_call_target="tpu_custom_call" | custom-call | tf_op jit(solution)/shard_map/exchange/pallas_call | solution.py:468
  37.1 1.7 %copy.12 = f32[32,32,768]{2,1,0:T(8,128)} copy(f32[32,32,768]{2,1,0:T(8,128)S(1)} %get-tuple-element.2) | data formatting | bytes 6291456
  38.8 0.7 %copy.13 = f32[8,8,768]{2,1,0:T(8,128)} copy(f32[8,8,768]{2,1,0:T(8,128)S(1)} %get-tuple-element.3) | data formatting | bytes 393216

commit v5 on v4

--- a/solution.py
+++ b/solution.py
@@ -16,10 +16,11 @@
 SLOTS = 512
 FACES = 2048
 GRP, BLK = 8, 16
-ROWS = WX * WY * ZB
+LANES = 192
+ROWS = WX * WY * NZ // LANES
 PACK = 4
 SINK = 4
-CUTS = (24, 0, 3)
+CUTS = (12, 0, 4)
 
 
 def split3(v):
@@ -237,7 +238,9 @@
 
     target = target_v[...]
     target_xy = ((target >> 8) * 43691) >> 17
-    code = (((target >> 7) - 6 * target_xy) * (WX * WY) + target_xy) * 128 + (target & 127)
+    target_z = target - NZ * target_xy
+    part = ((target_z >> 6) * 43691) >> 17
+    code = (part * (WX * WY) + target_xy) * LANES + (target_z - LANES * part)
     fields = list(split3(tf_s[...])) + list(split3(cond_v[...]))
     fields += [((code >> 8) << 8).astype(F32), (code & 255).astype(F32)]
     many = jnp.concatenate([jnp.where(mine, f, 0.0).astype(BF) for f in fields], axis=0)
@@ -288,14 +291,13 @@
         kp[0, x] = k0 * r
         kp[1, x] = k1 * r
         kp[2, x] = k2 * r
-    for zb in range(ZB):
-        for x in range(WX):
-            at = zb * 64 + x * 8
-            dep[at:at + 8, 0:128] = cur[0, x + 1, 8:16, zb * 128:(zb + 1) * 128]
-    across = dep[:, 0:128].T
-    for i, part in enumerate(split3(across)):
-        table[i * 128:(i + 1) * 128, :] = part.astype(BF)
-    dep[...] = jnp.zeros((ROWS, 256), F32)
+    block = jnp.concatenate([cur[0, x + 1, 8:16, :] for x in range(WX)], axis=0)
+    quarters = [block if q == 0 else pltpu.roll(block, NZ - LANES * q, 1) for q in range(4)]
+    halves = [jnp.concatenate([quarters[q][:, :256], quarters[q + 1][:, :256]], axis=0).T for q in (0, 2)]
+    across = jnp.concatenate([h[:LANES] for h in halves], axis=1)
+    for i, piece in enumerate(split3(across)):
+        table[i * LANES:(i + 1) * LANES, :] = piece.astype(BF)
+    dep[...] = jnp.zeros((2 * LANES, ROWS), F32)
 
     for i in range(8, 10):
         loads[i].wait()
@@ -336,11 +338,9 @@
     def slabs(i, carry):
         return slab(2 * i + 1, slab(2 * i, carry))
 
-    lax.fori_loop(0, 6, slabs, 0)
+    lax.fori_loop(0, 4, slabs, 0)
     send("t", "g")
-    send("v", "g")
-
-    lax.fori_loop(6, CUTS[0] // 2, slabs, 0)
+    lax.fori_loop(4, CUTS[0] // 2, slabs, 0)
 
     own_at = pl.ds(b, 1)
     inc[own_at] = snd[own_at]
@@ -354,17 +354,18 @@
 
         field = [jnp.concatenate([inc[i][:, f * SLOTS:(f + 1) * SLOTS] for i in src], axis=1) for f in range(3)]
         code = field[2].astype(I32)
-        hot = onehot(code >> 7, ROWS)
-        mask = lax.broadcasted_iota(I32, (128, PACK * SLOTS), 0) == (code & 127)
+        row = ((code >> 6) * 43691) >> 17
+        hot = onehot(row, ROWS)
+        mask = lax.broadcasted_iota(I32, (LANES, PACK * SLOTS), 0) == code - LANES * row
         found = dot(table[...], hot)
-        found = found[0:128] + found[128:256] + found[256:384]
+        found = found[0:LANES] + found[LANES:2 * LANES] + found[2 * LANES:]
         wall = jnp.sum(jnp.where(mask, found, 0.0), axis=0, keepdims=True)
         flux = field[1] * (field[0] - wall)
         hi = flux.astype(BF).astype(F32)
         spread = jnp.concatenate([jnp.where(mask, hi, 0.0), jnp.where(mask, flux - hi, 0.0)], axis=0)
         for j, i in enumerate(src):
             flx[i] = flux[:, j * SLOTS:(j + 1) * SLOTS]
-        dep[...] += dot_nt(hot, spread.astype(BF))
+        dep[...] += dot_nt(spread.astype(BF), hot)
         for i in src:
             @pl.when(i != b)
             def _():
@@ -382,10 +383,17 @@
         return base[x] + beside
 
     solid_receive(0)
+    summed = dep[0:LANES, :] + dep[LANES:, :]
+    summed = jnp.concatenate([summed, jnp.zeros((256 - LANES, ROWS), F32)], axis=0)
+    deposits = jnp.zeros((WX * WY, NZ), F32)
+    for h in range(2):
+        half = summed[:, h * 128:(h + 1) * 128].T
+        for p in range(2):
+            wide = jnp.concatenate([half[p * 64:(p + 1) * 64], jnp.zeros((WX * WY, NZ - 256), F32)], axis=1)
+            q = 2 * h + p
+            deposits = deposits + (wide if q == 0 else pltpu.roll(wide, LANES * q, 1))
     for x in range(WX):
-        deposit = jnp.concatenate(
-            [dep[zb * 64 + x * 8:zb * 64 + x * 8 + 8, 0:128] + dep[zb * 64 + x * 8:zb * 64 + x * 8 + 8, 128:256]
-             for zb in range(ZB)], axis=1)
+        deposit = deposits[x * 8:x * 8 + 8]
         base[x] = (0.5 * cur[0, x + 1, 8:16, :] + deposit) * inv[x]
         cur[1, x + 1, 8:16, :] = sweep(0, x)
     solid_send(1)
@@ -404,6 +412,7 @@
         return carry
 
     lax.fori_loop(1, BLK, returned, 0)
+    send("v", "g")
     for j in range(BLK):
         rmat[j:j + 1, :] = ret[j]
     stacked = jnp.concatenate(list(split3(rmat[...])), axis=0).astype(BF)
@@ -422,11 +431,6 @@
         return carry
 
     lax.fori_loop(0, NX, edge, 0)
-    receive("t", "g")
-    receive("v", "g")
-    adv[0] += 0.1 * face(xrcv[0, 0], temp(0, slice(0, NY)), xrcv[0, 1], vx[0])
-    adv[NX - 1] -= 0.1 * face(temp(NX - 1, slice(0, NY)), xrcv[1, 0], vx[NX - 1], xrcv[1, 1])
-
     def sink_group(i, carry):
         total = sink(i, weights, rowcode)
         for x in range(SINK):
@@ -442,6 +446,11 @@
         cur[3, x + 1, 8:16, :] = sweep(2, x)
     solid_send(3)
     lax.fori_loop(CUTS[2], NX // SINK, sink_group, 0)
+    receive("t", "g")
+    receive("v", "g")
+    adv[0] += 0.1 * face(xrcv[0, 0], temp(0, slice(0, NY)), xrcv[0, 1], vx[0])
+    adv[NX - 1] -= 0.1 * face(temp(NX - 1, slice(0, NY)), xrcv[1, 0], vx[NX - 1], xrcv[1, 1])
+
     solid_receive(3)
     for x in range(WX):
         solid_out[x] = sweep(3, x)
@@ -497,8 +506,8 @@
             pltpu.VMEM((3, WX, WY, NZ), F32),
             pltpu.VMEM((WX, WY, NZ), F32),
             pltpu.VMEM((WX, WY, NZ), F32),
-            pltpu.VMEM((3 * 128, ROWS), BF),
-            pltpu.VMEM((ROWS, 256), F32),
+            pltpu.VMEM((3 * LANES, ROWS), BF),
+            pltpu.VMEM((2 * LANES, ROWS), F32),
             pltpu.VMEM((NX, NZ), F32),
             pltpu.VMEM((NY, NZ), F32),
             pltpu.VMEM((256, FACES), BF),

time: 39.6 us -> 37.3 us (0.942)
  Pallas kernels: 36.5 us -> 34.1 us
    pallas_call x1, Pallas kernels: 36.5 us -> 34.1 us  [shards(): pl.pallas_call(main_kernel, out_shape=(pltpu.VMEM((NX, NY, NZ), F32), plt...]
where the time goes in v5:
time: 37.3 us; the launch traced here: 37.1 us
  Pallas kernels  34.1 us (91%)
  local copies, waits for them, and re-layouts  2.34 us (6%)
  between operations  0.64 us (2%)
    pallas_call x1, Pallas kernels, shards(): pl.pallas_call(main_kernel, out_shape=(pltpu.VMEM((NX, NY, NZ), F32), plt...  34.1 us
    unnamed x2, local copies, waits for them, and re-layouts  2.34 us

profile of v5, /device:TPU:14, one launch (start us, length us, event | category | flops | bytes accessed | tf_op | source)
XLA Modules:
  0.0 37.1 jit_solution(7532826636187073061)
XLA Ops:
  0.6 34.1 %exchange.1 = (f32[32,32,768]{2,1,0:T(8,128)S(1)}, f32[8,8,768]{2,1,0:T(8,128)S(1)}) custom-call(s32[1,2048]{1,0:T(1,128)} %cell_v.1, s32[1,2048]{1,0:T(1,128)} %owner_v.1, s32[1,2048]{1,0:T(1,128)} %target_v.1, f32[1,2048]{1,0:T(1,128)} %cond_v.1, f32[32,32,768]{2,1,0:T(8,128)} %fluid.1, f32[3,32,32,768]{3,2,1,0:T(8,128)} %vel.1, f32[8,8,768]{2,1,0:T(8,128)} %solid.1, ...), custom_call_target="tpu_custom_call" | custom-call | tf_op jit(solution)/shard_map/exchange/pallas_call | solution.py:477
  34.8 1.7 %copy.12 = f32[32,32,768]{2,1,0:T(8,128)} copy(f32[32,32,768]{2,1,0:T(8,128)S(1)} %get-tuple-element.2) | data formatting | bytes 6291456
  36.4 0.7 %copy.13 = f32[8,8,768]{2,1,0:T(8,128)} copy(f32[8,8,768]{2,1,0:T(8,128)S(1)} %get-tuple-element.3) | data formatting | bytes 393216

commit v6 on v5

--- a/solution.py
+++ b/solution.py
@@ -19,8 +19,8 @@
 LANES = 192
 ROWS = WX * WY * NZ // LANES
 PACK = 4
-SINK = 4
-CUTS = (12, 0, 4)
+SINK = 8
+CUTS = (12, 2)
 
 
 def split3(v):
@@ -78,12 +78,12 @@
 
 
 def main_kernel(
-    cell_v, owner_v, target_v, cond_v, fluid, vel, solid, kond,
+    cell_h, owner_h, target_h, cond_h, fluid, vel, solid, kond,
     adv, solid_out,
-    rows_v, rows_s,
+    cell_v, owner_v, target_v, cond_v, rows_v, rows_s,
     tg, vy, vx, vz, buf, tf_s, rank_s, snd, inc, flx, ret, rmat,
     xrcv, ysnd, yrcv, cur, sysnd, syrcv, kp, inv, base, table, dep, gs, gxs, weights, rowcode,
-    lsem, ssem, rsem, osem, isem, fsem, bsem,
+    lsem, rsmall, ssem, rsem, osem, isem, fsem, bsem,
 ):
     g = lax.axis_index("grp")
     b = lax.axis_index("blk")
@@ -93,6 +93,52 @@
         step = 1 if side else -1
         return (g + step, b) if axis == "g" else (g, b + step)
 
+    loads = []
+
+    def load(src, dst):
+        c = pltpu.make_async_copy(src, dst, lsem.at[len(loads)])
+        c.start()
+        loads.append(c)
+
+    small = []
+    for i, (src, dst) in enumerate(((cell_h, cell_v), (owner_h, owner_v), (target_h, target_v), (cond_h, cond_v))):
+        c = pltpu.make_async_copy(src, dst, rsmall.at[i])
+        c.start()
+        small.append(c)
+    load(solid, cur.at[0, pl.ds(1, WX), pl.ds(8, WY), :])
+    for zb in range(ZB):
+        load(fluid.at[:, :, pl.ds(zb * 128, 128)], tg.at[zb])
+
+    def temp(x, rows):
+        return jnp.concatenate([tg[zb, x, rows, :] for zb in range(ZB)], axis=1)
+
+    bar = pltpu.get_barrier_semaphore()
+
+    def greet(k, carry):
+        pl.semaphore_signal(bar, inc=1, device_id=(g, lax.rem(b + k, BLK)), device_id_type=MESH)
+        return carry
+
+    lax.fori_loop(1, BLK, greet, 0)
+    for side in (0, 1):
+        @pl.when(has["g", side])
+        def _():
+            pl.semaphore_signal(bar, inc=1, device_id=neighbour("g", side), device_id_type=MESH)
+
+    for side in (0, 1):
+        @pl.when(jnp.logical_not(has["g", side]))
+        def _():
+            xrcv[side] = jnp.zeros((2, NY, NZ), F32)
+            wat = 0 if side == 0 else WX + 1
+            for k in range(4):
+                cur[k, wat, 8:16, :] = jnp.zeros((WY, NZ), F32)
+
+        @pl.when(jnp.logical_not(has["b", side]))
+        def _():
+            yrcv[side] = jnp.zeros((2, NX, NZ), F32)
+            for k in range(4):
+                syrcv[k, side] = jnp.zeros((WX, NZ), F32)
+
+    small[0].wait()
     cell = cell_v[...]
     cell_xy = ((cell >> 8) * 43691) >> 17
     cell_row = ((cell >> 7) - 6 * cell_xy) * (NX * NY) + cell_xy
@@ -100,46 +146,7 @@
         rows_v[c:c + 1, :] = cell_row[:, c * 128:(c + 1) * 128]
     rows_copy = pltpu.make_async_copy(rows_v, rows_s, lsem.at[14])
     rows_copy.start()
-    loads = []
-
-    def load(src, dst):
-        c = pltpu.make_async_copy(src, dst, lsem.at[len(loads)])
-        c.start()
-        loads.append(c)
-
-    load(solid, cur.at[0, pl.ds(1, WX), pl.ds(8, WY), :])
-    for zb in range(ZB):
-        load(fluid.at[:, :, pl.ds(zb * 128, 128)], tg.at[zb])
-
-    def temp(x, rows):
-        return jnp.concatenate([tg[zb, x, rows, :] for zb in range(ZB)], axis=1)
-
-    bar = pltpu.get_barrier_semaphore()
-
-    def greet(k, carry):
-        pl.semaphore_signal(bar, inc=1, device_id=(g, lax.rem(b + k, BLK)), device_id_type=MESH)
-        return carry
-
-    lax.fori_loop(1, BLK, greet, 0)
-    for side in (0, 1):
-        @pl.when(has["g", side])
-        def _():
-            pl.semaphore_signal(bar, inc=1, device_id=neighbour("g", side), device_id_type=MESH)
-
-    for side in (0, 1):
-        @pl.when(jnp.logical_not(has["g", side]))
-        def _():
-            xrcv[side] = jnp.zeros((2, NY, NZ), F32)
-            wat = 0 if side == 0 else WX + 1
-            for k in range(4):
-                cur[k, wat, 8:16, :] = jnp.zeros((WY, NZ), F32)
-
-        @pl.when(jnp.logical_not(has["b", side]))
-        def _():
-            yrcv[side] = jnp.zeros((2, NX, NZ), F32)
-            for k in range(4):
-                syrcv[k, side] = jnp.zeros((WX, NZ), F32)
-
+    small[1].wait()
     owner = owner_v[...]
     own16 = onehot(owner, BLK)
     upper = jnp.where(
@@ -236,6 +243,8 @@
         lane = cell_v[:, cols] & 127
         tf_s[:, cols] = jnp.sum(jnp.where(lane128 == lane, block, 0.0), axis=0, keepdims=True)
 
+    small[2].wait()
+    small[3].wait()
     target = target_v[...]
     target_xy = ((target >> 8) * 43691) >> 17
     target_z = target - NZ * target_xy
@@ -283,6 +292,49 @@
 
     lax.fori_loop(0, NX, pack, 0)
     send("y", "b")
+    for i in range(8, 10):
+        loads[i].wait()
+    gxs[...] = jnp.zeros((NY, NZ), F32)
+    sub = lax.broadcasted_iota(I32, (8, NZ), 0)
+
+    def slab(x, carry, end=False):
+        def finish(t, lower, upper):
+            r = 8 * t
+            here = temp(x, slice(r, r + 8))
+            total = gxs[r:r + 8, :] + (lower - upper)
+            if not end:
+                high = face(here, temp(x + 1, slice(r, r + 8)), vx[x, r:r + 8, :], vx[x + 1, r:r + 8, :])
+                total = total - high
+                gxs[r:r + 8, :] = high
+            v = vz[x, r:r + 8, :]
+            bottom = face(shift_up(here, lane), here, shift_up(v, lane), v)
+            last = face(here[:, -128:], 0.0, v[:, -128:], 0.0)
+            top = shift_down(bottom, lane, last)
+            adv[x, r:r + 8, :] = here + 0.1 * (total + (bottom - top))
+
+        zero = jnp.zeros((8, NZ), F32)
+        temp0 = vel0 = low = low_up = zero
+        for t in range(4):
+            r = 8 * t
+            here, v = temp(x, slice(r, r + 8)), vy[x, r:r + 8, :]
+            temp1, vel1 = pltpu.roll(here, 1, 0), pltpu.roll(v, 1, 0)
+            g_t = face(jnp.where(sub == 0, temp0, temp1), here, jnp.where(sub == 0, vel0, vel1), v)
+            if t == 0:
+                g_t = jnp.where(sub == 0, 0.0, g_t)
+            g_up = pltpu.roll(g_t, 7, 0)
+            if t > 0:
+                finish(t - 1, low, jnp.where(sub == 7, g_up, low_up))
+            temp0, vel0, low, low_up = temp1, vel1, g_t, g_up
+        finish(3, low, jnp.where(sub == 7, 0.0, low_up))
+        return carry
+
+    def slabs(i, carry):
+        return slab(2 * i + 1, slab(2 * i, carry))
+
+    lax.fori_loop(0, 4, slabs, 0)
+    send("t", "g")
+    lax.fori_loop(4, CUTS[0] // 2, slabs, 0)
+
     loads[10].wait()
     for x in range(WX):
         k0, k1, k2 = kp[0, x], kp[1, x], kp[2, x]
@@ -298,49 +350,6 @@
     for i, piece in enumerate(split3(across)):
         table[i * LANES:(i + 1) * LANES, :] = piece.astype(BF)
     dep[...] = jnp.zeros((2 * LANES, ROWS), F32)
-
-    for i in range(8, 10):
-        loads[i].wait()
-    gxs[...] = jnp.zeros((NY, NZ), F32)
-    sub = lax.broadcasted_iota(I32, (8, NZ), 0)
-
-    def slab(x, carry, end=False):
-        def finish(t, lower, upper):
-            r = 8 * t
-            here = temp(x, slice(r, r + 8))
-            total = gxs[r:r + 8, :] + (lower - upper)
-            if not end:
-                high = face(here, temp(x + 1, slice(r, r + 8)), vx[x, r:r + 8, :], vx[x + 1, r:r + 8, :])
-                total = total - high
-                gxs[r:r + 8, :] = high
-            v = vz[x, r:r + 8, :]
-            bottom = face(shift_up(here, lane), here, shift_up(v, lane), v)
-            last = face(here[:, -128:], 0.0, v[:, -128:], 0.0)
-            top = shift_down(bottom, lane, last)
-            adv[x, r:r + 8, :] = here + 0.1 * (total + (bottom - top))
-
-        zero = jnp.zeros((8, NZ), F32)
-        temp0 = vel0 = low = low_up = zero
-        for t in range(4):
-            r = 8 * t
-            here, v = temp(x, slice(r, r + 8)), vy[x, r:r + 8, :]
-            temp1, vel1 = pltpu.roll(here, 1, 0), pltpu.roll(v, 1, 0)
-            g_t = face(jnp.where(sub == 0, temp0, temp1), here, jnp.where(sub == 0, vel0, vel1), v)
-            if t == 0:
-                g_t = jnp.where(sub == 0, 0.0, g_t)
-            g_up = pltpu.roll(g_t, 7, 0)
-            if t > 0:
-                finish(t - 1, low, jnp.where(sub == 7, g_up, low_up))
-            temp0, vel0, low, low_up = temp1, vel1, g_t, g_up
-        finish(3, low, jnp.where(sub == 7, 0.0, low_up))
-        return carry
-
-    def slabs(i, carry):
-        return slab(2 * i + 1, slab(2 * i, carry))
-
-    lax.fori_loop(0, 4, slabs, 0)
-    send("t", "g")
-    lax.fori_loop(4, CUTS[0] // 2, slabs, 0)
 
     own_at = pl.ds(b, 1)
     inc[own_at] = snd[own_at]
@@ -440,12 +449,12 @@
                 adv[i * SINK + x, :, cols] += total[at:at + 32, :]
         return carry
 
-    lax.fori_loop(0, CUTS[2], sink_group, 0)
+    lax.fori_loop(0, CUTS[1], sink_group, 0)
     solid_receive(2)
     for x in range(WX):
         cur[3, x + 1, 8:16, :] = sweep(2, x)
     solid_send(3)
-    lax.fori_loop(CUTS[2], NX // SINK, sink_group, 0)
+    lax.fori_loop(CUTS[1], NX // SINK, sink_group, 0)
     receive("t", "g")
     receive("v", "g")
     adv[0] += 0.1 * face(xrcv[0, 0], temp(0, slice(0, NY)), xrcv[0, 1], vx[0])
@@ -480,9 +489,13 @@
             pltpu.VMEM((NX, NY, NZ), F32),
             pltpu.VMEM((WX, WY, NZ), F32),
         ),
-        in_specs=[vmem] * 4 + [hbm] * 4,
+        in_specs=[hbm] * 8,
         out_specs=(vmem, vmem),
         scratch_shapes=[
+            pltpu.VMEM((1, FACES), I32),
+            pltpu.VMEM((1, FACES), I32),
+            pltpu.VMEM((1, FACES), I32),
+            pltpu.VMEM((1, FACES), F32),
             pltpu.VMEM((FACES // 128, 128), I32),
             pltpu.SMEM((FACES // 128, 128), I32),
             pltpu.VMEM((ZB, NX, NY, 128), F32),
@@ -512,7 +525,7 @@
             pltpu.VMEM((NY, NZ), F32),
             pltpu.VMEM((256, FACES), BF),
             pltpu.VMEM((1, FACES), I32),
-            dma((15,)), dma((22,)), dma((22,)), dma((BLK,)), dma((BLK,)), dma((BLK,)), dma((BLK,)),
+            dma((15,)), dma((4,)), dma((22,)), dma((22,)), dma((BLK,)), dma((BLK,)), dma((BLK,)), dma((BLK,)),
         ],
         compiler_params=pltpu.CompilerParams(
             collective_id=0, has_side_effects=True, vmem_limit_bytes=60 * 1024 * 1024),

time: 37.3 us -> 36.5 us (0.979)
  Pallas kernels: 34.1 us -> 33.3 us
    pallas_call x1, Pallas kernels: 34.1 us -> 33.3 us  [shards(): pl.pallas_call(main_kernel, out_shape=(pltpu.VMEM((NX, NY, NZ), F32), plt...]
where the time goes in v6:
time: 36.5 us; the launch traced here: 36.3 us
  Pallas kernels  33.3 us (91%)
  local copies, waits for them, and re-layouts  2.34 us (6%)
  between operations  0.64 us (2%)
    pallas_call x1, Pallas kernels, shards(): pl.pallas_call(main_kernel, out_shape=(pltpu.VMEM((NX, NY, NZ), F32), plt...  33.3 us
    unnamed x2, local copies, waits for them, and re-layouts  2.34 us

profile of v6, /device:TPU:14, one launch (start us, length us, event | category | flops | bytes accessed | tf_op | source)
XLA Modules:
  0.0 36.3 jit_solution(1971237535114632809)
XLA Ops:
  0.6 33.3 %exchange.1 = (f32[32,32,768]{2,1,0:T(8,128)S(1)}, f32[8,8,768]{2,1,0:T(8,128)S(1)}) custom-call(s32[1,2048]{1,0:T(1,128)} %cell_h.1, s32[1,2048]{1,0:T(1,128)} %owner_h.1, s32[1,2048]{1,0:T(1,128)} %target_h.1, f32[1,2048]{1,0:T(1,128)} %cond_h.1, f32[32,32,768]{2,1,0:T(8,128)} %fluid.1, f32[3,32,32,768]{3,2,1,0:T(8,128)} %vel.1, f32[8,8,768]{2,1,0:T(8,128)} %solid.1, ...), custom_call_target="tpu_custom_call" | custom-call | tf_op jit(solution)/shard_map/exchange/pallas_call | solution.py:486
  34.0 1.7 %copy.12 = f32[32,32,768]{2,1,0:T(8,128)} copy(f32[32,32,768]{2,1,0:T(8,128)S(1)} %get-tuple-element.2) | data formatting | bytes 6291456
  35.7 0.7 %copy.13 = f32[8,8,768]{2,1,0:T(8,128)} copy(f32[8,8,768]{2,1,0:T(8,128)S(1)} %get-tuple-element.3) | data formatting | bytes 393216
